TPU v7x, 128 devices: a whole 4x4x4 slice. The times are simulated.
128 devices in a mesh: tile: 16 (over y, x), slab: 8 (over z, core).
Axes of the slice: x: 4, y: 4, z: 4, core: 2. Of those that a mesh axis runs over, the one named last changes fastest.
Arguments:
- intensities: bfloat16 [1792, 256, 256], P(('tile', 'slab')), may hold values from 0 to 0.5
- object_field: float32 [2, 2, 4096, 384], P(None, None, ('tile', 'slab')), may hold values from -3 to 3
- probe_wave: float32 [256, 512], replicated, may hold values from -6 to 6
- owner_tile: int32 [1792], replicated, may hold values from 0 to 15, as said below
- row_offset: int32 [1792], replicated, may hold values from 0 to 255
- col_offset: int32 [1792], replicated, may hold values from 0 to 1
Outputs:
- gradient: float32 [2, 2, 4096, 384], P(None, None, ('tile', 'slab'))
Inputs may be any that keep to these rules, and one draw needn't show every extreme that they name: `owner_tile`: read row r is read by device r // 14 of the tile+slab order. Among the 16 devices of one slab index, the rows of one device name one tile at most 2 times, and each tile is named by at most 16 of their rows; some tile reaches 16 and some device reaches 2 for some tile, for every slab index.
All inputs are finite; a program needn't handle non-finite values.
Results may differ from a plain program's by a relative error of at most 0.006.
The roundings to bfloat16 on the way count: a program that leaves them out, or rounds other values in their place, can miss the bound.
Values may be sent and summed in bfloat16 or wider, within the bound.
A program may use at most 64 MiB of HBM per device.

v0:
```python
import math

import jax
import jax.numpy as jnp
from jax import lax
from jax.sharding import PartitionSpec as P

COL_STEP = 128
K = 16
CAP = 2


chirp_strength = 40.0


def passed_along(value, axis, steps):
    count = lax.axis_size(axis)
    pairs = [(source, (source + steps) % count) for source in range(count)]
    return lax.ppermute(value, axis, pairs)


def make_tables(extent):
    counter = jnp.arange(extent, dtype=jnp.int32)
    product_index = counter[:, None] * counter[None, :] % extent
    angles = product_index.astype(jnp.float32) * (2.0 * math.pi / extent)
    scaling = 1.0 / math.sqrt(extent)
    cosine = (jnp.cos(angles) * scaling).astype(jnp.bfloat16)
    sine_part = (jnp.sin(angles) * scaling).astype(jnp.bfloat16)
    forward = jnp.concatenate(
        [jnp.concatenate([cosine, -sine_part], 1), jnp.concatenate([sine_part, cosine], 1)], 0
    )
    inverse = jnp.concatenate(
        [jnp.concatenate([cosine, sine_part], 1), jnp.concatenate([-sine_part, cosine], 1)], 0
    )
    frequency = ((counter + extent // 2) % extent - extent // 2).astype(jnp.float32) / extent
    phases = chirp_strength * (frequency[:, None] ** 2 + frequency[None, :] ** 2)
    kernel = jnp.concatenate([jnp.cos(phases), -jnp.sin(phases)], 1)
    return (cosine, sine_part, forward, inverse, kernel)


def transform(field, tables, backward):
    cosine, sine_part, forward, inverse, kernel = tables
    extent = cosine.shape[0]
    halfway = jnp.dot(
        field, inverse if backward else forward, preferred_element_type=jnp.float32
    ).astype(jnp.bfloat16)
    with_cosine = jnp.dot(cosine, halfway, preferred_element_type=jnp.float32)
    with_sine = jnp.dot(sine_part, halfway, preferred_element_type=jnp.float32)
    if backward:
        real_part = with_cosine[:, :extent] - with_sine[:, extent:]
        imag_part = with_cosine[:, extent:] + with_sine[:, :extent]
    else:
        real_part = with_cosine[:, :extent] + with_sine[:, extent:]
        imag_part = with_cosine[:, extent:] - with_sine[:, :extent]
    return jnp.concatenate([real_part, imag_part], 1)


def complex_product(left, right, conjugate):
    extent = left.shape[1] // 2
    left_real = left[:, :extent]
    left_imag = -left[:, extent:] if conjugate else left[:, extent:]
    right_real = right[:, :extent]
    right_imag = right[:, extent:]
    return jnp.concatenate(
        [
            left_real * right_real - left_imag * right_imag,
            left_real * right_imag + left_imag * right_real,
        ],
        1,
    )


def position_gradient(window, probe_wave, measured, tables):
    kernel = tables[4]
    extent = measured.shape[0]
    layers = window.shape[0]
    pieces = [
        jnp.concatenate([window[slice_index, 0], window[slice_index, 1]], 1)
        for slice_index in range(layers)
    ]
    incoming = [probe_wave]
    entering = complex_product(probe_wave, pieces[0], False).astype(jnp.bfloat16)
    slice_index = 1
    spread_wave = complex_product(kernel, transform(entering, tables, False), False).astype(
        jnp.bfloat16
    )
    arrived = transform(spread_wave, tables, True)
    incoming.append(arrived)
    entering = complex_product(arrived, pieces[slice_index], False).astype(jnp.bfloat16)
    farfield = transform(entering, tables, False)
    modelled = farfield[:, :extent] ** 2 + farfield[:, extent:] ** 2
    misfit = modelled - measured.astype(jnp.float32)
    far_grad = (farfield * jnp.concatenate([misfit, misfit], 1)).astype(jnp.bfloat16)
    exit_grad = transform(far_grad, tables, True)
    slice_terms = [None] * layers
    for slice_index in range(layers - 1, -1, -1):
        slice_terms[slice_index] = complex_product(incoming[slice_index], exit_grad, True)
        if slice_index > 0:
            back_wave = complex_product(pieces[slice_index], exit_grad, True).astype(jnp.bfloat16)
            back_spread = complex_product(kernel, transform(back_wave, tables, False), True).astype(
                jnp.bfloat16
            )
            exit_grad = transform(back_spread, tables, True)
    return jnp.stack(
        [jnp.stack([one_term[:, :extent], one_term[:, extent:]]) for one_term in slice_terms]
    )


def send_ranks(column_group):
    reads_dev = column_group.shape[1]
    counter = jnp.arange(reads_dev, dtype=jnp.int32)
    earlier = counter[None, :] < counter[:, None]
    matching = column_group[:, :, None] == column_group[:, None, :]
    return jnp.sum((matching & earlier[None]).astype(jnp.int32), 2, dtype=jnp.int32)


def arrivals(column_group, order_set, tile_here, slab_number, slab_count, capacity):
    tile_count = column_group.shape[0]
    reads_dev = column_group.shape[1]
    sender = jnp.arange(tile_count, dtype=jnp.int32)[:, None]
    position = jnp.arange(reads_dev, dtype=jnp.int32)[None, :]
    ours = (column_group == tile_here).reshape(-1)
    landing = (sender * capacity + order_set).reshape(-1)
    read_row = ((sender * slab_count + slab_number) * reads_dev + position).reshape(-1)
    buffer_index = jnp.arange(tile_count * capacity, dtype=jnp.int32)
    matched = ours[None, :] & (landing[None, :] == buffer_index[:, None])
    active_position = jnp.any(matched, 1)
    slot_row = jnp.sum(jnp.where(matched, read_row[None, :], 0), 1, dtype=jnp.int32)
    return (active_position, slot_row)


def compact_order(active_position, space_count):
    live_flags = active_position.astype(jnp.int32)
    before = jnp.cumsum(live_flags, dtype=jnp.int32) - live_flags
    wanted = jnp.arange(space_count, dtype=jnp.int32)
    return active_position[None, :] & (before[None, :] == wanted[:, None])


def shards(intensities, object_field, probe_wave, owner_tile, row_offset, col_offset):
    tile_count = lax.axis_size("tile")
    slab_count = lax.axis_size("slab")
    tile_here = lax.axis_index("tile")
    slab_here = lax.axis_index("slab")
    reads_dev = intensities.shape[0]
    extent = intensities.shape[1]
    pixels = extent * extent
    capacity = CAP
    space_count = K
    owner_table = owner_tile.reshape(tile_count, slab_count, reads_dev)
    columns = lax.dynamic_index_in_dim(owner_table, slab_here, 1, keepdims=False)
    send_order = send_ranks(columns)
    my_dest = lax.dynamic_index_in_dim(columns, tile_here, 0, keepdims=False)
    my_rank = lax.dynamic_index_in_dim(send_order, tile_here, 0, keepdims=False)
    target = my_dest * capacity + my_rank
    buffer_index = jnp.arange(tile_count * capacity, dtype=jnp.int32)
    packing = (buffer_index[:, None] == target[None, :]).astype(jnp.bfloat16)
    outgoing = jnp.dot(
        packing, intensities.reshape(reads_dev, pixels), preferred_element_type=jnp.float32
    ).astype(jnp.bfloat16)
    received = lax.all_to_all(outgoing, "tile", split_axis=0, concat_axis=0, tiled=True)
    local_active, rows_here = arrivals(
        columns, send_order, tile_here, slab_here, slab_count, capacity
    )
    local_choice = compact_order(local_active, space_count)
    patterns = jnp.dot(
        local_choice.astype(jnp.bfloat16), received, preferred_element_type=jnp.float32
    ).astype(jnp.bfloat16)
    pattern_rows = jnp.sum(jnp.where(local_choice, rows_here[None, :], 0), 1, dtype=jnp.int32)
    pattern_count = jnp.sum(local_active.astype(jnp.int32), dtype=jnp.int32)
    own_rows = lax.all_gather(object_field, "slab", axis=2, tiled=True)
    next_part = passed_along(own_rows, "tile", -1)
    extended = jnp.concatenate([own_rows, next_part], 2)
    tables = make_tables(extent)
    depth = object_field.shape[0]
    images = patterns.reshape(space_count, extent, extent)

    def accumulate(item_number, totals):
        source_row = lax.dynamic_index_in_dim(pattern_rows, item_number, 0, keepdims=False)
        top_row = lax.dynamic_index_in_dim(row_offset, source_row, 0, keepdims=False)
        left_col = lax.dynamic_index_in_dim(col_offset, source_row, 0, keepdims=False) * COL_STEP
        zero_index = jnp.zeros((), jnp.int32)
        starting = (zero_index, zero_index, top_row, left_col)
        window = lax.dynamic_slice(extended, starting, (depth, 2, extent, extent))
        measured = lax.dynamic_index_in_dim(images, item_number, 0, keepdims=False)
        gradient_part = position_gradient(window, probe_wave, measured, tables)
        current = lax.dynamic_slice(totals, starting, (depth, 2, extent, extent))
        return lax.dynamic_update_slice(totals, current + gradient_part, starting)

    totals = lax.fori_loop(0, pattern_count, accumulate, jnp.zeros(extended.shape, jnp.float32))
    tile_height = own_rows.shape[2]
    lower = totals[:, :, tile_height:]
    padding = jnp.zeros((depth, 2, tile_height - extent, totals.shape[3]), jnp.float32)
    moved = passed_along(lower, "tile", 1)
    combined = totals[:, :, :tile_height] + jnp.concatenate([moved, padding], 2)
    return lax.psum_scatter(combined, "slab", scatter_dimension=2, tiled=True)


def solution(mesh):
    placed = (
        P(("tile", "slab"), None, None),
        P(None, None, ("tile", "slab"), None),
        P(),
        P(),
        P(),
        P(),
    )
    return jax.shard_map(
        shards,
        mesh=mesh,
        in_specs=placed,
        out_specs=P(None, None, ("tile", "slab"), None),
        check_vma=False,
    )
```

profile of v0, /device:TPU:1, one launch (start us, length us, event | category | flops | bytes accessed | tf_op | source)
XLA Modules:
  0.0 989.2 jit_solution(254745163554753798)
XLA Ops:
  6.5 1.8 copy.42
  12.9 3.2 convolution_convert_fusion.6
  16.1 5.9 all_to_all.8
  22.0 7.8 all-to-all-start
  30.3 7.0 all-gather.2.cloned.1.call-done
  37.3 4.6 collective-permute-start
  48.1 48.7 %all-to-all-done = bf16[16,2,65536]{2,1,0:T(2,128)(2,1)} async-done(((bf16[16,2,65536]{2,1,0:T(2,128)(2,1)}), bf16[16,2,65536]{2,1,0:T(2,128)(2,1)}, u32[]{:S(2)}, u32[]{:S(2)}) %all-to-all-start) | async-done | bytes 4194336 | tf_op jit(solution)/shard_map/all_to_all | solution.py:160
  96.8 5.4 all_to_all.10
  102.2 2.9 convolution_convert_fusion.7
  105.1 1.8 copy.60
  106.9 17.1 %collective-permute-done = f32[2,2,256,384]{3,1,0,2:T(2,128)S(1)} collective-permute-done((f32[2,2,256,384]{3,1,0,2:T(2,128)}, f32[2,2,256,384]{3,1,0,2:T(2,128)S(1)}, u32[]{:S(2)}, u32[]{:S(2)}) %collective-permute-start) | collective-permute-done | bytes 1572896 | tf_op jit(solution)/shard_map/ppermute | solution.py:19
  124.0 3.0 pad_maximum_fusion
  127.0 1.9 broadcast_in_dim.22.clone
  128.9 799.1 %while.14 = (s32[]{:T(128)}, f32[2,2,512,384]{3,2,1,0:T(8,128)}, s32[]{:T(128)}, s32[16]{0:T(128)S(1)}, s32[1792]{0:T(1024)}, /*index=5*/s32[1792]{0:T(1024)}, f...) while((s32[]{:T(128)}, f32[2,2,512,384]{3,2,1,0:T(8,128)}, ...), condition=%wide.region_7.8_spmd.clone.clone.clone, body=%wide.region_6.7_spmd.clone.clone.clone.sunk | while | flops 1632960512 | bytes 54661596 | solution.py:189
  138.6 3.0 constant_dynamic-slice_fusion.12
  169.1 10.1 %dynamic_update_slice.8 = f32[2,2,512,384]{3,2,1,0:T(8,128)} dynamic-update-slice(f32[2,2,512,384]{3,2,1,0:T(8,128)} %get-tuple-element.613, f32[2,2,256,256]{3,2,1,0:T(8,128)S(1)} %copy.74, s32[]{:T(128)} %constant.106.clone.1..sunk, s32[]{:T(128)} %constant.106.clone.1..sunk, s32[]{:T(128)S(6)} %select_n.222, s32[]{:T(128)S(6)} %select_n.223) | dynamic-update-slice | bytes 2097156 | tf_op jit(solution)/shard_map/while/body/dynamic_update_slice | solution.py:187
  188.7 2.9 constant_dynamic-slice_fusion.12
  219.2 10.5 %dynamic_update_slice.8 = f32[2,2,512,384]{3,2,1,0:T(8,128)} dynamic-update-slice(f32[2,2,512,384]{3,2,1,0:T(8,128)} %get-tuple-element.613, f32[2,2,256,256]{3,2,1,0:T(8,128)S(1)} %copy.74, s32[]{:T(128)} %constant.106.clone.1..sunk, s32[]{:T(128)} %constant.106.clone.1..sunk, s32[]{:T(128)S(6)} %select_n.222, s32[]{:T(128)S(6)} %select_n.223) | dynamic-update-slice | bytes 2097156 | tf_op jit(solution)/shard_map/while/body/dynamic_update_slice | solution.py:187
  239.2 2.9 constant_dynamic-slice_fusion.12
  269.8 10.4 %dynamic_update_slice.8 = f32[2,2,512,384]{3,2,1,0:T(8,128)} dynamic-update-slice(f32[2,2,512,384]{3,2,1,0:T(8,128)} %get-tuple-element.613, f32[2,2,256,256]{3,2,1,0:T(8,128)S(1)} %copy.74, s32[]{:T(128)} %constant.106.clone.1..sunk, s32[]{:T(128)} %constant.106.clone.1..sunk, s32[]{:T(128)S(6)} %select_n.222, s32[]{:T(128)S(6)} %select_n.223) | dynamic-update-slice | bytes 2097156 | tf_op jit(solution)/shard_map/while/body/dynamic_update_slice | solution.py:187
  289.7 3.0 constant_dynamic-slice_fusion.12
  320.3 10.4 %dynamic_update_slice.8 = f32[2,2,512,384]{3,2,1,0:T(8,128)} dynamic-update-slice(f32[2,2,512,384]{3,2,1,0:T(8,128)} %get-tuple-element.613, f32[2,2,256,256]{3,2,1,0:T(8,128)S(1)} %copy.74, s32[]{:T(128)} %constant.106.clone.1..sunk, s32[]{:T(128)} %constant.106.clone.1..sunk, s32[]{:T(128)S(6)} %select_n.222, s32[]{:T(128)S(6)} %select_n.223) | dynamic-update-slice | bytes 2097156 | tf_op jit(solution)/shard_map/while/body/dynamic_update_slice | solution.py:187
  340.2 3.0 constant_dynamic-slice_fusion.12
  370.8 9.8 dynamic_update_slice.8
  390.0 3.0 constant_dynamic-slice_fusion.12
  420.7 9.4 dynamic_update_slice.8
  439.6 2.9 constant_dynamic-slice_fusion.12
  470.1 10.5 %dynamic_update_slice.8 = f32[2,2,512,384]{3,2,1,0:T(8,128)} dynamic-update-slice(f32[2,2,512,384]{3,2,1,0:T(8,128)} %get-tuple-element.613, f32[2,2,256,256]{3,2,1,0:T(8,128)S(1)} %copy.74, s32[]{:T(128)} %constant.106.clone.1..sunk, s32[]{:T(128)} %constant.106.clone.1..sunk, s32[]{:T(128)S(6)} %select_n.222, s32[]{:T(128)S(6)} %select_n.223) | dynamic-update-slice | bytes 2097156 | tf_op jit(solution)/shard_map/while/body/dynamic_update_slice | solution.py:187
  490.1 3.0 constant_dynamic-slice_fusion.12
  520.7 9.6 dynamic_update_slice.8
  539.8 3.0 constant_dynamic-slice_fusion.12
  570.4 10.0 %dynamic_update_slice.8 = f32[2,2,512,384]{3,2,1,0:T(8,128)} dynamic-update-slice(f32[2,2,512,384]{3,2,1,0:T(8,128)} %get-tuple-element.613, f32[2,2,256,256]{3,2,1,0:T(8,128)S(1)} %copy.74, s32[]{:T(128)} %constant.106.clone.1..sunk, s32[]{:T(128)} %constant.106.clone.1..sunk, s32[]{:T(128)S(6)} %select_n.222, s32[]{:T(128)S(6)} %select_n.223) | dynamic-update-slice | bytes 2097156 | tf_op jit(solution)/shard_map/while/body/dynamic_update_slice | solution.py:187
  589.9 3.0 constant_dynamic-slice_fusion.12
  620.6 9.6 dynamic_update_slice.8
  639.6 3.1 constant_dynamic-slice_fusion.12
  670.2 9.4 dynamic_update_slice.8
  689.1 3.0 constant_dynamic-slice_fusion.12
  719.7 9.8 dynamic_update_slice.8
  739.0 3.0 constant_dynamic-slice_fusion.12
  769.6 8.2 dynamic_update_slice.8
  787.3 3.1 constant_dynamic-slice_fusion.12
  818.0 9.3 dynamic_update_slice.8
  836.7 3.0 constant_dynamic-slice_fusion.12
  867.3 9.9 dynamic_update_slice.8
  886.6 3.0 constant_dynamic-slice_fusion.12
  917.2 9.9 %dynamic_update_slice.8 = f32[2,2,512,384]{3,2,1,0:T(8,128)} dynamic-update-slice(f32[2,2,512,384]{3,2,1,0:T(8,128)} %get-tuple-element.613, f32[2,2,256,256]{3,2,1,0:T(8,128)S(1)} %copy.74, s32[]{:T(128)} %constant.106.clone.1..sunk, s32[]{:T(128)} %constant.106.clone.1..sunk, s32[]{:T(128)S(6)} %select_n.222, s32[]{:T(128)S(6)} %select_n.223) | dynamic-update-slice | bytes 2097156 | tf_op jit(solution)/shard_map/while/body/dynamic_update_slice | solution.py:187
  929.8 22.6 %collective-permute-done.1 = f32[2,2,256,384]{3,2,1,0:T(8,128)S(1)} collective-permute-done((f32[2,2,256,384]{3,2,1,0:T(8,128)S(1)}, f32[2,2,256,384]{3,2,1,0:T(8,128)S(1)}, u32[]{:S(2)}, u32[]{:S(2)}) %collective-permute-start.1) | collective-permute-done | bytes 1572896 | tf_op jit(solution)/shard_map/ppermute | solution.py:19
  953.7 28.7 %reduce-scatter.2.cloned.1.call-done = f32[2,2,32,384]{3,2,1,0:T(8,128)} async-done(((f32[2,2,256,384]{3,2,1,0:T(8,128)}), f32[2,2,32,384]{3,2,1,0:T(8,128)}) %reduce-scatter.2.cloned.1.call-update) | async-done | bytes 196624 | tf_op jit(solution)/shard_map/reduce_scatter | solution.py:195
  (765 shorter events, 522.4 us)
Async XLA Ops:
  6.5 30.8 %all-gather.2.cloned.1.call-start = ((), (), s32[]{:S(2)}) async-start(), calls=%async_computation.2 | async-start | bytes 1769472 | tf_op jit(solution)/shard_map/all_gather | solution.py:170
  22.0 20.3 %copy-start.2 = (f32[256,512]{1,0:T(8,128)S(1)}, f32[256,512]{1,0:T(8,128)}, u32[]{:S(2)}) copy-start(f32[256,512]{1,0:T(8,128)} %param.10) | copy-start | bytes 1572868
  22.0 74.8 %all-to-all-start = ((bf16[16,2,65536]{2,1,0:T(2,128)(2,1)}), bf16[16,2,65536]{2,1,0:T(2,128)(2,1)}, u32[]{:S(2)}, u32[]{:S(2)}) async-start(bf16[16,2,65536]{2,1,0:T(2,128)(2,1)} %all_to_all.8), calls=%async_computation | async-start | bytes 8388608 | tf_op jit(solution)/shard_map/all_to_all | solution.py:160
  29.7 952.7 %reduce-scatter.2.cloned.1.call-start = ((), (), s32[]{:S(2)}) async-start(), calls=%async_computation.3 | async-start | bytes 1769472 | tf_op jit(solution)/shard_map/reduce_scatter | solution.py:195
  37.3 86.7 %collective-permute-start = (f32[2,2,256,384]{3,1,0,2:T(2,128)}, f32[2,2,256,384]{3,1,0,2:T(2,128)S(1)}, u32[]{:S(2)}, u32[]{:S(2)}) collective-permute-start(f32[2,2,256,384]{3,1,0,2:T(2,128)} %all-gather.2.cloned.1.call-done), channel_id=1, source_target_pairs={{0,120},{8,0},{16,8},{24,16},{32,24},{40,32},{48,40},{56,48},{64,5... | collective-permute-start | bytes 4718600 | tf_op jit(solution)/shard_map/ppermute | solution.py:19
  105.1 18.9 %copy-start.1 = (f32[2,2,256,384]{3,1,0,2:T(2,128)S(1)}, f32[2,2,256,384]{3,1,0,2:T(2,128)}, u32[]{:S(2)}) copy-start(f32[2,2,256,384]{3,1,0,2:T(2,128)} %all-gather.2.cloned.1.call-done) | copy-start | bytes 4718596
  129.7 33.1 %copy-start.3 = (bf16[512,512]{1,0:T(8,128)(2,1)}, bf16[512,512]{1,0:T(8,128)(2,1)S(1)}, u32[]{:S(2)}) copy-start(bf16[512,512]{1,0:T(8,128)(2,1)S(1)} %get-tuple-element.642) | copy-start | bytes 1572868 | tf_op jit(solution)/shard_map/while
  168.8 10.4 %copy-start.4 = (bf16[512,512]{1,0:T(8,128)(2,1)S(1)}, bf16[512,512]{1,0:T(8,128)(2,1)}, u32[]{:S(2)}) copy-start(bf16[512,512]{1,0:T(8,128)(2,1)} %copy-done.3) | copy-start | bytes 1572868 | tf_op jit(solution)/shard_map/while
  179.9 33.1 %copy-start.3 = (bf16[512,512]{1,0:T(8,128)(2,1)}, bf16[512,512]{1,0:T(8,128)(2,1)S(1)}, u32[]{:S(2)}) copy-start(bf16[512,512]{1,0:T(8,128)(2,1)S(1)} %get-tuple-element.642) | copy-start | bytes 1572868 | tf_op jit(solution)/shard_map/while
  218.9 10.9 %copy-start.4 = (bf16[512,512]{1,0:T(8,128)(2,1)S(1)}, bf16[512,512]{1,0:T(8,128)(2,1)}, u32[]{:S(2)}) copy-start(bf16[512,512]{1,0:T(8,128)(2,1)} %copy-done.3) | copy-start | bytes 1572868 | tf_op jit(solution)/shard_map/while
  230.4 33.1 %copy-start.3 = (bf16[512,512]{1,0:T(8,128)(2,1)}, bf16[512,512]{1,0:T(8,128)(2,1)S(1)}, u32[]{:S(2)}) copy-start(bf16[512,512]{1,0:T(8,128)(2,1)S(1)} %get-tuple-element.642) | copy-start | bytes 1572868 | tf_op jit(solution)/shard_map/while
  269.5 10.8 %copy-start.4 = (bf16[512,512]{1,0:T(8,128)(2,1)S(1)}, bf16[512,512]{1,0:T(8,128)(2,1)}, u32[]{:S(2)}) copy-start(bf16[512,512]{1,0:T(8,128)(2,1)} %copy-done.3) | copy-start | bytes 1572868 | tf_op jit(solution)/shard_map/while
  280.9 33.1 %copy-start.3 = (bf16[512,512]{1,0:T(8,128)(2,1)}, bf16[512,512]{1,0:T(8,128)(2,1)S(1)}, u32[]{:S(2)}) copy-start(bf16[512,512]{1,0:T(8,128)(2,1)S(1)} %get-tuple-element.642) | copy-start | bytes 1572868 | tf_op jit(solution)/shard_map/while
  319.9 10.8 %copy-start.4 = (bf16[512,512]{1,0:T(8,128)(2,1)S(1)}, bf16[512,512]{1,0:T(8,128)(2,1)}, u32[]{:S(2)}) copy-start(bf16[512,512]{1,0:T(8,128)(2,1)} %copy-done.3) | copy-start | bytes 1572868 | tf_op jit(solution)/shard_map/while
  331.3 33.2 %copy-start.3 = (bf16[512,512]{1,0:T(8,128)(2,1)}, bf16[512,512]{1,0:T(8,128)(2,1)S(1)}, u32[]{:S(2)}) copy-start(bf16[512,512]{1,0:T(8,128)(2,1)S(1)} %get-tuple-element.642) | copy-start | bytes 1572868 | tf_op jit(solution)/shard_map/while
  370.4 10.1 %copy-start.4 = (bf16[512,512]{1,0:T(8,128)(2,1)S(1)}, bf16[512,512]{1,0:T(8,128)(2,1)}, u32[]{:S(2)}) copy-start(bf16[512,512]{1,0:T(8,128)(2,1)} %copy-done.3) | copy-start | bytes 1572868 | tf_op jit(solution)/shard_map/while
  381.2 33.2 %copy-start.3 = (bf16[512,512]{1,0:T(8,128)(2,1)}, bf16[512,512]{1,0:T(8,128)(2,1)S(1)}, u32[]{:S(2)}) copy-start(bf16[512,512]{1,0:T(8,128)(2,1)S(1)} %get-tuple-element.642) | copy-start | bytes 1572868 | tf_op jit(solution)/shard_map/while
  420.3 9.8 copy-start.4
  430.7 33.1 %copy-start.3 = (bf16[512,512]{1,0:T(8,128)(2,1)}, bf16[512,512]{1,0:T(8,128)(2,1)S(1)}, u32[]{:S(2)}) copy-start(bf16[512,512]{1,0:T(8,128)(2,1)S(1)} %get-tuple-element.642) | copy-start | bytes 1572868 | tf_op jit(solution)/shard_map/while
  469.8 10.9 %copy-start.4 = (bf16[512,512]{1,0:T(8,128)(2,1)S(1)}, bf16[512,512]{1,0:T(8,128)(2,1)}, u32[]{:S(2)}) copy-start(bf16[512,512]{1,0:T(8,128)(2,1)} %copy-done.3) | copy-start | bytes 1572868 | tf_op jit(solution)/shard_map/while
  481.3 33.2 %copy-start.3 = (bf16[512,512]{1,0:T(8,128)(2,1)}, bf16[512,512]{1,0:T(8,128)(2,1)S(1)}, u32[]{:S(2)}) copy-start(bf16[512,512]{1,0:T(8,128)(2,1)S(1)} %get-tuple-element.642) | copy-start | bytes 1572868 | tf_op jit(solution)/shard_map/while
  520.4 10.0 %copy-start.4 = (bf16[512,512]{1,0:T(8,128)(2,1)S(1)}, bf16[512,512]{1,0:T(8,128)(2,1)}, u32[]{:S(2)}) copy-start(bf16[512,512]{1,0:T(8,128)(2,1)} %copy-done.3) | copy-start | bytes 1572868 | tf_op jit(solution)/shard_map/while
  531.0 33.1 %copy-start.3 = (bf16[512,512]{1,0:T(8,128)(2,1)}, bf16[512,512]{1,0:T(8,128)(2,1)S(1)}, u32[]{:S(2)}) copy-start(bf16[512,512]{1,0:T(8,128)(2,1)S(1)} %get-tuple-element.642) | copy-start | bytes 1572868 | tf_op jit(solution)/shard_map/while
  570.1 10.4 %copy-start.4 = (bf16[512,512]{1,0:T(8,128)(2,1)S(1)}, bf16[512,512]{1,0:T(8,128)(2,1)}, u32[]{:S(2)}) copy-start(bf16[512,512]{1,0:T(8,128)(2,1)} %copy-done.3) | copy-start | bytes 1572868 | tf_op jit(solution)/shard_map/while
  581.1 33.2 %copy-start.3 = (bf16[512,512]{1,0:T(8,128)(2,1)}, bf16[512,512]{1,0:T(8,128)(2,1)S(1)}, u32[]{:S(2)}) copy-start(bf16[512,512]{1,0:T(8,128)(2,1)S(1)} %get-tuple-element.642) | copy-start | bytes 1572868 | tf_op jit(solution)/shard_map/while
  620.2 9.9 %copy-start.4 = (bf16[512,512]{1,0:T(8,128)(2,1)S(1)}, bf16[512,512]{1,0:T(8,128)(2,1)}, u32[]{:S(2)}) copy-start(bf16[512,512]{1,0:T(8,128)(2,1)} %copy-done.3) | copy-start | bytes 1572868 | tf_op jit(solution)/shard_map/while
  630.8 33.2 %copy-start.3 = (bf16[512,512]{1,0:T(8,128)(2,1)}, bf16[512,512]{1,0:T(8,128)(2,1)S(1)}, u32[]{:S(2)}) copy-start(bf16[512,512]{1,0:T(8,128)(2,1)S(1)} %get-tuple-element.642) | copy-start | bytes 1572868 | tf_op jit(solution)/shard_map/while
  669.9 9.8 copy-start.4
  680.3 33.1 %copy-start.3 = (bf16[512,512]{1,0:T(8,128)(2,1)}, bf16[512,512]{1,0:T(8,128)(2,1)S(1)}, u32[]{:S(2)}) copy-start(bf16[512,512]{1,0:T(8,128)(2,1)S(1)} %get-tuple-element.642) | copy-start | bytes 1572868 | tf_op jit(solution)/shard_map/while
  719.4 10.1 %copy-start.4 = (bf16[512,512]{1,0:T(8,128)(2,1)S(1)}, bf16[512,512]{1,0:T(8,128)(2,1)}, u32[]{:S(2)}) copy-start(bf16[512,512]{1,0:T(8,128)(2,1)} %copy-done.3) | copy-start | bytes 1572868 | tf_op jit(solution)/shard_map/while
  730.2 33.1 %copy-start.3 = (bf16[512,512]{1,0:T(8,128)(2,1)}, bf16[512,512]{1,0:T(8,128)(2,1)S(1)}, u32[]{:S(2)}) copy-start(bf16[512,512]{1,0:T(8,128)(2,1)S(1)} %get-tuple-element.642) | copy-start | bytes 1572868 | tf_op jit(solution)/shard_map/while
  769.2 8.6 copy-start.4
  778.5 33.2 %copy-start.3 = (bf16[512,512]{1,0:T(8,128)(2,1)}, bf16[512,512]{1,0:T(8,128)(2,1)S(1)}, u32[]{:S(2)}) copy-start(bf16[512,512]{1,0:T(8,128)(2,1)S(1)} %get-tuple-element.642) | copy-start | bytes 1572868 | tf_op jit(solution)/shard_map/while
  817.6 9.6 copy-start.4
  827.9 33.1 %copy-start.3 = (bf16[512,512]{1,0:T(8,128)(2,1)}, bf16[512,512]{1,0:T(8,128)(2,1)S(1)}, u32[]{:S(2)}) copy-start(bf16[512,512]{1,0:T(8,128)(2,1)S(1)} %get-tuple-element.642) | copy-start | bytes 1572868 | tf_op jit(solution)/shard_map/while
  867.0 10.2 %copy-start.4 = (bf16[512,512]{1,0:T(8,128)(2,1)S(1)}, bf16[512,512]{1,0:T(8,128)(2,1)}, u32[]{:S(2)}) copy-start(bf16[512,512]{1,0:T(8,128)(2,1)} %copy-done.3) | copy-start | bytes 1572868 | tf_op jit(solution)/shard_map/while
  877.8 33.1 %copy-start.3 = (bf16[512,512]{1,0:T(8,128)(2,1)}, bf16[512,512]{1,0:T(8,128)(2,1)S(1)}, u32[]{:S(2)}) copy-start(bf16[512,512]{1,0:T(8,128)(2,1)S(1)} %get-tuple-element.642) | copy-start | bytes 1572868 | tf_op jit(solution)/shard_map/while
  916.8 10.3 %copy-start.4 = (bf16[512,512]{1,0:T(8,128)(2,1)S(1)}, bf16[512,512]{1,0:T(8,128)(2,1)}, u32[]{:S(2)}) copy-start(bf16[512,512]{1,0:T(8,128)(2,1)} %copy-done.3) | copy-start | bytes 1572868 | tf_op jit(solution)/shard_map/while
  928.0 24.4 %copy-start = (f32[2,2,512,384]{3,2,1,0:T(8,128)S(1)}, f32[2,2,512,384]{3,2,1,0:T(8,128)}, u32[]{:S(2)}) copy-start(f32[2,2,512,384]{3,2,1,0:T(8,128)} %get-tuple-element.198) | copy-start | bytes 9437188
  929.7 22.7 %collective-permute-start.1 = (f32[2,2,256,384]{3,2,1,0:T(8,128)S(1)}, f32[2,2,256,384]{3,2,1,0:T(8,128)S(1)}, u32[]{:S(2)}, u32[]{:S(2)}) collective-permute-start(f32[2,2,256,384]{3,2,1,0:T(8,128)S(1)} %slice.133), channel_id=1, source_target_pairs={{0,8},{8,16},{16,24},{24,32},{32,40},{40,48},{48,56},{56,64},{64,7... | collective-permute-start | bytes 4718600 | tf_op jit(solution)/shard_map/ppermute | solution.py:19
Sparse Core Ops, SparseCore 0:
  9.0 28.2 all-gather.1
  953.8 28.5 reduce-scatter.1
where the time goes:
time: 1000 us; the launch traced here: 989 us
  local copies, waits for them, and re-layouts  344 us (34%)
  matrix products  313 us (31%)
  waiting for transfers between devices  124 us (12%)
  other arithmetic  95.7 us (10%)
  loops' own time  86.1 us (9%)
  between operations  13.6 us (1%)
  starting transfers between devices  12.5 us (1%)
    dynamic_update_slice x32, local copies, waits for them, and re-layouts, accumulate(): return lax.dynamic_update_slice(totals, current + gradient_part, starting)  162 us
    dot_general x96, matrix products, transform(): with_sine = jnp.dot(sine_part, halfway, preferred_element_type=jnp.float32)  114 us
    dot_general x96, matrix products, transform(): with_cosine = jnp.dot(cosine, halfway, preferred_element_type=jnp.float32)  113 us
    another operation x1, loops' own time, shards(): lax.fori_loop(0, pattern_count, accumulate, jnp.zeros(extended.shape, jnp...  86.1 us
    dot_general x96, matrix products, transform(): jnp.dot(field, inverse if backward else forward, preferred_element_type=j...  80.5 us
    another operation x98, other arithmetic  62.3 us
    all_to_all x1, waiting for transfers between devices, shards(): lax.all_to_all(outgoing, 'tile', split_axis=0, concat_axis=0, tiled=True)  48.7 us
    slice x16, local copies, waits for them, and re-layouts, position_gradient(): window[slice_index, 0]  47.9 us
  transfers between devices with their start and end apart: 5, of which 5 were waited for; matrix products, arithmetic and copies ran while one was open for 2% of the time, Pallas kernels for 0%

commit v1 on v0

v1 whole, which is shorter than its diff:
```python
import functools
import math

import jax
import jax.numpy as jnp
import numpy as np
from jax import lax
from jax.experimental import pallas as pl
from jax.experimental.pallas import tpu as pltpu
from jax.sharding import PartitionSpec as P

bf16 = jnp.bfloat16
f32 = jnp.float32
MESH = pl.DeviceIdType.MESH
K = 16
CAP = 2
COL_STEP = 128
CHIRP = 40.0
LANES = 128
CHUNK = 64
VMEM_LIMIT = 60 * 2**20

smem = pl.BlockSpec(memory_space=pltpu.SMEM)
vmem = pl.BlockSpec(memory_space=pltpu.VMEM)
anyspace = pl.BlockSpec(memory_space=pl.ANY)


def make_tables(n):
    count = np.arange(n)
    angles = ((count[:, None] * count[None, :]) % n).astype(np.float32)
    angles = angles * np.float32(2.0 * math.pi / n)
    scale = np.float32(1.0 / math.sqrt(n))
    c = np.cos(angles) * scale
    s = np.sin(angles) * scale
    forward = np.block([[c, -s], [s, c]]).astype(np.float32)
    inverse = np.block([[c, s], [-s, c]]).astype(np.float32)
    f = (((count + n // 2) % n) - n // 2).astype(np.float32) / np.float32(n)
    phases = np.float32(CHIRP) * (f[:, None] ** 2 + f[None, :] ** 2)
    kernel = np.stack([np.cos(phases), -np.sin(phases)]).astype(np.float32)
    return jnp.asarray(forward, bf16), jnp.asarray(inverse, bf16), jnp.asarray(kernel)


def pack_kernel(tiles, slabs, reads, owner, rowoff, coloff, images, field,
                packed, count, slot, row, col, shard, hold, used, insem, outsem):
    tile = lax.axis_index("tile")
    slab = lax.axis_index("slab")
    for k in range(reads):
        pltpu.make_async_copy(images.at[k], hold.at[k], insem.at[k]).start()
    for t in range(tiles):
        used[t] = 0
    for k in range(reads):
        dest = owner[(tile * slabs + slab) * reads + k]
        rank = used[dest]
        used[dest] = rank + 1
        pltpu.make_async_copy(images.at[k], hold.at[k], insem.at[k]).wait()
        pltpu.make_async_copy(hold.at[k], packed.at[dest, rank], outsem.at[k]).start()
    for s in range(2):
        for q in range(2):
            for h in range(3):
                shard[2 * s + q, h] = field[s, q, :, h * LANES:(h + 1) * LANES]

    def sender(i, found):
        base = (i * slabs + slab) * reads

        def one(k, state):
            n, rank = state
            hit = owner[base + k] == tile
            slot[n] = i * CAP + rank
            row[n] = rowoff[base + k]
            col[n] = coloff[base + k]
            step = hit.astype(jnp.int32)
            return n + step, rank + step

        return lax.fori_loop(0, reads, one, (found, jnp.int32(0)), unroll=True)[0]

    count[0] = lax.fori_loop(0, tiles, sender, jnp.int32(0))
    for k in range(reads):
        pltpu.make_async_copy(hold.at[k], packed.at[0, 0], outsem.at[k]).wait()


def pack(owner, rowoff, coloff, images, field, tiles, slabs):
    reads, n, _ = images.shape
    rows = field.shape[2]
    return pl.pallas_call(
        functools.partial(pack_kernel, tiles, slabs, reads),
        out_shape=(
            jax.ShapeDtypeStruct((tiles, CAP, n, n), bf16),
            jax.ShapeDtypeStruct((1,), jnp.int32),
            jax.ShapeDtypeStruct((K + 1,), jnp.int32),
            jax.ShapeDtypeStruct((K + 1,), jnp.int32),
            jax.ShapeDtypeStruct((K + 1,), jnp.int32),
            jax.ShapeDtypeStruct((4, 3, rows, LANES), f32),
        ),
        in_specs=[smem, smem, smem, anyspace, vmem],
        out_specs=(anyspace, smem, smem, smem, smem, vmem),
        scratch_shapes=[
            pltpu.VMEM((reads, n, n), bf16),
            pltpu.SMEM((tiles,), jnp.int32),
            pltpu.SemaphoreType.DMA((reads,)),
            pltpu.SemaphoreType.DMA((reads,)),
        ],
        name="pack",
    )(owner, rowoff, coloff, images, field)


def exchange_kernel(tiles, slabs, rows, packed, shard, got, field,
                    hold, localsem, psend, precv, nsend, nrecv, asend, arecv, bsend, brecv):
    tile = lax.axis_index("tile")
    slab = lax.axis_index("slab")
    before = lax.rem(tile + tiles - 1, tiles)
    barrier = pltpu.get_barrier_semaphore()
    for d in range(1, tiles):
        peer = lax.rem(tile + d, tiles)
        pl.semaphore_signal(barrier, inc=1, device_id={"tile": peer, "slab": slab}, device_id_type=MESH)
    for d in range(1, slabs):
        peer = lax.rem(slab + d, slabs)
        pl.semaphore_signal(barrier, inc=1, device_id={"tile": tile, "slab": peer}, device_id_type=MESH)
    pl.semaphore_wait(barrier, tiles - 1 + slabs - 1)

    height = rows * slabs
    mine = field.at[:, :, pl.ds(pl.multiple_of(slab * rows, rows), rows), :]
    after = field.at[:, :, pl.ds(pl.multiple_of(height + slab * rows, rows), rows), :]
    copies = []

    def push(src, dst, send, recv, t, s):
        copy = pltpu.make_async_remote_copy(
            src_ref=src, dst_ref=dst, send_sem=send, recv_sem=recv,
            device_id={"tile": t, "slab": s}, device_id_type=MESH,
        )
        copy.start()
        return copy

    ahead = push(shard, after, nsend, nrecv, before, slab)
    for d in range(1, slabs):
        copies.append(push(shard, mine, asend.at[d - 1], arecv.at[d - 1], tile, lax.rem(slab + d, slabs)))
    for d in range(1, tiles):
        peer = lax.rem(tile + d, tiles)
        copies.append(push(packed.at[peer], got.at[tile], psend.at[d - 1], precv.at[d - 1], peer, slab))
    keep = pltpu.make_async_copy(shard, mine, localsem.at[0])
    keep.start()
    first = pltpu.make_async_copy(packed.at[tile], hold, localsem.at[1])
    first.start()
    first.wait()
    second = pltpu.make_async_copy(hold, got.at[tile], localsem.at[1])
    second.start()
    ahead.wait()
    for d in range(1, slabs):
        copies.append(push(after, after, bsend.at[d - 1], brecv.at[d - 1], tile, lax.rem(slab + d, slabs)))
    second.wait()
    keep.wait()
    for copy in copies:
        copy.wait()


def exchange(packed, shard, tiles, slabs):
    _, _, n, _ = packed.shape
    planes, cols, rows, lanes = shard.shape
    sem = pltpu.SemaphoreType.DMA
    return pl.pallas_call(
        functools.partial(exchange_kernel, tiles, slabs, rows),
        out_shape=(
            jax.ShapeDtypeStruct(packed.shape, packed.dtype),
            jax.ShapeDtypeStruct((planes, cols, 2 * rows * slabs, lanes), shard.dtype),
        ),
        in_specs=[anyspace, vmem],
        out_specs=(anyspace, anyspace),
        scratch_shapes=[
            pltpu.VMEM((CAP, n, n), bf16),
            sem((2,)),
            sem((tiles - 1,)), sem((tiles - 1,)),
            sem, sem,
            sem((slabs - 1,)), sem((slabs - 1,)),
            sem((slabs - 1,)), sem((slabs - 1,)),
        ],
        compiler_params=pltpu.CompilerParams(collective_id=0, has_side_effects=True),
        name="exchange",
    )(packed, shard)


def grad_kernel(count, slot, row, col, field, images, probe, forward, inverse, kernel,
                total, x, h, y, wave, image, imsem):
    n = 256
    total[...] = jnp.zeros_like(total)

    def fetch(i):
        index = slot[i]
        return pltpu.make_async_copy(
            images.at[lax.div(index, CAP), lax.rem(index, CAP)], image.at[lax.rem(i, 2)], imsem.at[lax.rem(i, 2)]
        )

    def transform(backward):
        right = inverse if backward else forward
        left = forward if backward else inverse
        half = jnp.dot(x[...], right[...], preferred_element_type=f32)
        h[:n, :] = half[:, :n].astype(bf16)
        h[n:, :] = half[:, n:].astype(bf16)
        y[...] = jnp.dot(left[...], h[...], preferred_element_type=f32)

    def product(ar, ai, br, bi):
        return ar * br - ai * bi, ar * bi + ai * br

    def conjugate_product(ar, ai, br, bi):
        return ar * br + ai * bi, ar * bi - ai * br

    def step(i, carry):
        top = row[i]
        left = col[i]
        fetch(i).wait()

        @pl.when(i + 1 < count[0])
        def _():
            fetch(i + 1).start()

        def window(s, q, r, c):
            return field[2 * s + q, left + c, pl.ds(top + r, CHUNK), :].astype(f32)

        def add(s, r, c, re, im):
            total[2 * s, left + c, pl.ds(top + r, CHUNK), :] += re
            total[2 * s + 1, left + c, pl.ds(top + r, CHUNK), :] += im

        def put(r, c, parts):
            x[r:r + CHUNK, c * LANES:(c + 1) * LANES] = parts[0].astype(bf16)
            x[r:r + CHUNK, n + c * LANES:n + (c + 1) * LANES] = parts[1].astype(bf16)

        def pieces():
            for r in range(0, n, CHUNK):
                for c in range(2):
                    yield r, c, slice(r, r + CHUNK), slice(n + r, n + r + CHUNK), slice(c * LANES, (c + 1) * LANES)

        for r, c, a, b, l in pieces():
            put(r, c, product(probe[a, l], probe[a, n + c * LANES:n + (c + 1) * LANES], window(0, 0, r, c), window(0, 1, r, c)))
        transform(False)
        for r, c, a, b, l in pieces():
            put(r, c, product(kernel[0, a, l], kernel[1, a, l], y[a, l], y[b, l]))
        transform(True)
        for r, c, a, b, l in pieces():
            re, im = y[a, l], y[b, l]
            wave[a, l] = re
            wave[b, l] = im
            put(r, c, product(re, im, window(1, 0, r, c), window(1, 1, r, c)))
        transform(False)
        for r, c, a, b, l in pieces():
            re, im = y[a, l], y[b, l]
            misfit = re * re + im * im - image[lax.rem(i, 2), a, l].astype(f32)
            put(r, c, (re * misfit, im * misfit))
        transform(True)
        for r, c, a, b, l in pieces():
            re, im = y[a, l], y[b, l]
            add(1, r, c, *conjugate_product(wave[a, l], wave[b, l], re, im))
            put(r, c, conjugate_product(window(1, 0, r, c), window(1, 1, r, c), re, im))
        transform(False)
        for r, c, a, b, l in pieces():
            put(r, c, conjugate_product(kernel[0, a, l], kernel[1, a, l], y[a, l], y[b, l]))
        transform(True)
        for r, c, a, b, l in pieces():
            add(0, r, c, *conjugate_product(probe[a, l], probe[a, n + c * LANES:n + (c + 1) * LANES], y[a, l], y[b, l]))
        return carry

    @pl.when(count[0] > 0)
    def _():
        fetch(0).start()

    lax.fori_loop(0, count[0], step, 0)


def gradient(count, slot, row, col, field, images, probe):
    n = probe.shape[0]
    forward, inverse, kernel = make_tables(n)
    return pl.pallas_call(
        grad_kernel,
        out_shape=jax.ShapeDtypeStruct(field.shape, f32),
        in_specs=[smem] * 4 + [vmem, anyspace] + [vmem] * 4,
        out_specs=vmem,
        scratch_shapes=[
            pltpu.VMEM((n, 2 * n), bf16),
            pltpu.VMEM((2 * n, n), bf16),
            pltpu.VMEM((2 * n, n), f32),
            pltpu.VMEM((2 * n, n), f32),
            pltpu.VMEM((2, n, n), bf16),
            pltpu.SemaphoreType.DMA((2,)),
        ],
        compiler_params=pltpu.CompilerParams(vmem_limit_bytes=VMEM_LIMIT),
        name="gradient",
    )(count, slot, row, col, field, images, probe, forward, inverse, kernel)


def reduce_kernel(tiles, slabs, cores, total, out, part, near, far, outgoing,
                  localsem, csend, crecv, zsend, zrecv, fsend, frecv):
    tile = lax.axis_index("tile")
    slab = lax.axis_index("slab")
    levels = slabs // cores
    core = lax.rem(slab, cores)
    level = lax.div(slab, cores)
    other = level * cores + (1 - core)
    following = lax.rem(tile + 1, tiles)
    preceding = lax.rem(tile + tiles - 1, tiles)
    barrier = pltpu.get_barrier_semaphore()

    def greet(t, s):
        pl.semaphore_signal(barrier, inc=1, device_id={"tile": t, "slab": s}, device_id_type=MESH)

    greet(tile, other)
    for d in range(1, levels):
        greet(tile, lax.rem(level + d, levels) * cores + core)
    for d in range(levels):
        place = lax.rem(level + d, levels) * cores + core
        greet(following, place)
        greet(preceding, place)
    pl.semaphore_wait(barrier, 1 + levels - 1 + 2 * levels)

    def block(which, d):
        return which * levels + lax.rem(level + d, levels)

    order = [(1, 2), (1, 1), (1, 3), (0, 2), (0, 1), (0, 3), (1, 0), (0, 0)]
    swaps = []
    takes = []
    for k, (which, d) in enumerate(order):
        b = block(which, d)
        copy = pltpu.make_async_remote_copy(
            src_ref=total.at[:, :, b, 1 - core], dst_ref=near.at[k], send_sem=csend.at[k], recv_sem=crecv.at[k],
            device_id={"tile": tile, "slab": other}, device_id_type=MESH,
        )
        copy.start()
        swaps.append(copy)
        take = pltpu.make_async_copy(total.at[:, :, b, core], part.at[k], localsem.at[k])
        take.start()
        takes.append(take)
    sends = []
    for k, (which, d) in enumerate(order):
        takes[k].wait()
        swaps[k].wait_recv()
        if (which, d) == (0, 0):
            continue
        outgoing[k] = (part[k] + near[k]).astype(bf16)
        place = lax.rem(level + d, levels) * cores + core
        if which == 0:
            copy = pltpu.make_async_remote_copy(
                src_ref=outgoing.at[k], dst_ref=far.at[d - 1], send_sem=zsend.at[d - 1], recv_sem=zrecv.at[d - 1],
                device_id={"tile": tile, "slab": place}, device_id_type=MESH,
            )
        else:
            copy = pltpu.make_async_remote_copy(
                src_ref=outgoing.at[k], dst_ref=far.at[levels - 1 + d], send_sem=fsend.at[d], recv_sem=frecv.at[d],
                device_id={"tile": following, "slab": place}, device_id_type=MESH,
            )
        copy.start()
        sends.append(copy)
    for copy in sends:
        copy.wait()
    for copy in swaps:
        copy.wait_send()
    last = len(order) - 1
    for p in range(4):
        for h in range(3):
            value = part[last, p, h] + near[last, p, h]
            for k in range(2 * levels - 1):
                value = value + far[k, p, h].astype(f32)
            out[p // 2, p % 2, :, h * LANES:(h + 1) * LANES] = value


def reduce(total, tiles, slabs):
    cores = 2
    levels = slabs // cores
    planes, cols, rows, lanes = total.shape
    each = rows // (2 * slabs)
    sem = pltpu.SemaphoreType.DMA
    total = total.reshape(planes, cols, 2 * levels, cores, each, lanes)
    count = 2 * levels
    return pl.pallas_call(
        functools.partial(reduce_kernel, tiles, slabs, cores),
        out_shape=jax.ShapeDtypeStruct((2, 2, each, cols * lanes), f32),
        in_specs=[anyspace],
        out_specs=vmem,
        scratch_shapes=[
            pltpu.VMEM((count, planes, cols, each, lanes), f32),
            pltpu.VMEM((count, planes, cols, each, lanes), f32),
            pltpu.VMEM((count - 1, planes, cols, each, lanes), bf16),
            pltpu.VMEM((count, planes, cols, each, lanes), bf16),
            sem((count,)),
            sem((count,)), sem((count,)),
            sem((levels - 1,)), sem((levels - 1,)),
            sem((levels,)), sem((levels,)),
        ],
        compiler_params=pltpu.CompilerParams(collective_id=1, has_side_effects=True, vmem_limit_bytes=VMEM_LIMIT),
        name="reduce",
    )(total)


def shards(intensities, object_field, probe_wave, owner_tile, row_offset, col_offset):
    tiles = lax.axis_size("tile")
    slabs = lax.axis_size("slab")
    packed, count, slot, row, col, shard = pack(
        owner_tile, row_offset, col_offset, intensities, object_field, tiles, slabs
    )
    images, field = exchange(packed, shard, tiles, slabs)
    total = gradient(count, slot, row, col, field, images, probe_wave)
    return reduce(total, tiles, slabs)


def solution(mesh):
    placed = (
        P(("tile", "slab"), None, None),
        P(None, None, ("tile", "slab"), None),
        P(),
        P(),
        P(),
        P(),
    )
    return jax.shard_map(
        shards,
        mesh=mesh,
        in_specs=placed,
        out_specs=P(None, None, ("tile", "slab"), None),
        check_vma=False,
    )
```

time: 1000 us -> 165 us (0.17)
  local copies, waits for them, and re-layouts: 344 us -> 1.62 us
  matrix products: 313 us -> 0 us
  Pallas kernels: 0 us -> 161 us
  waiting for transfers between devices: 124 us -> 0 us
  other arithmetic: 95.7 us -> 0 us
  loops' own time: 86.1 us -> 0 us
  between operations: 13.6 us -> 0.03 us
  starting transfers between devices: 12.5 us -> 0 us
    dot_general x290 -> x0, matrix products: 313 us -> none  [the longest x96 114 us: transform(): with_sine = jnp.dot(sine_part, halfway, preferred_element_type=jnp.float32)]
    dynamic_update_slice x32 -> x0, local copies, waits for them, and re-layouts: 162 us -> none  [accumulate(): return lax.dynamic_update_slice(totals, current + gradient_part, starting)]
    pallas_call x0 -> x4, Pallas kernels: none -> 161 us  [the longest x1 75.1 us: exchange(): pl.pallas_call(functools.partial(exchange_kernel, tiles, slabs, rows), ou...]
    dynamic_slice x112 -> x0, local copies, waits for them, and re-layouts: 101 us -> none  [the longest x32 31.1 us: accumulate(): current = lax.dynamic_slice(totals, starting, (depth, 2, extent, extent))]
    another operation x1 -> x0, loops' own time: 86.1 us -> none  [shards(): lax.fori_loop(0, pattern_count, accumulate, jnp.zeros(extended.shape, jnp...]
    another operation x146 -> x0, other arithmetic: 82.2 us -> none
    slice x17 -> x0, local copies, waits for them, and re-layouts: 49.6 us -> none  [the longest x16 47.9 us: position_gradient(): window[slice_index, 0]]
    all_to_all x1 -> x0, waiting for transfers between devices: 48.7 us -> none  [shards(): lax.all_to_all(outgoing, 'tile', split_axis=0, concat_axis=0, tiled=True)]
  transfers between devices with their start and end apart: 5 -> 0, of which waited for: 5 -> 0; matrix products, arithmetic and copies ran while one was open for 2% -> 0% of each run, Pallas kernels for 0% -> 0%
where the time goes in v1:
time: 165 us; the launch traced here: 163 us
  Pallas kernels  161 us (98%)
    pallas_call x1, Pallas kernels, exchange(): pl.pallas_call(functools.partial(exchange_kernel, tiles, slabs, rows), ou...  75.1 us
    pallas_call x1, Pallas kernels, gradient(): pl.pallas_call(grad_kernel, out_shape=jax.ShapeDtypeStruct(field.shape, f...  63.1 us
    pallas_call x1, Pallas kernels, reduce(): pl.pallas_call(functools.partial(reduce_kernel, tiles, slabs, cores), out...  18.2 us
    pallas_call x1, Pallas kernels, pack(): pl.pallas_call(functools.partial(pack_kernel, tiles, slabs, reads), out_s...  4.63 us

profile of v1, /device:TPU:1, one launch (start us, length us, event | category | flops | bytes accessed | tf_op | source)
XLA Modules:
  0.0 162.7 jit_solution(11500384372385166853)
XLA Ops:
  0.0 4.6 %pack.1 = (bf16[16,2,256,256]{3,2,1,0:T(8,128)(2,1)}, s32[1]{0:T(128)}, s32[17]{0:T(128)}, s32[17]{0:T(128)}, s32[17]{0:T(128)}, /*index=5*/f32[4,3,32,128]{3,2,1,0:T(8,128)}) custom-call(s32[1792]{0:T(1024)} %owner.1, s32[1792]{0:T(1024)} %rowoff.1, s32[1792]{0:T(1024)} %coloff.1, bf16[14,256,256]{2,1,0:T(8,128)(2,1)} %images.1, f32[2,2,32,384]{3,2,1,0:T(8,128)} %field.1), custom_call_target="tpu_custom_call" | custom-call | tf_op jit(solution)/shard_map/pack/pallas_call | solution.py:84
  4.6 75.1 %exchange.1 = (bf16[16,2,256,256]{3,2,1,0:T(8,128)(2,1)}, f32[4,3,512,128]{3,2,1,0:T(8,128)}) custom-call(bf16[16,2,256,256]{3,2,1,0:T(8,128)(2,1)} %get-tuple-element.17.packed, f32[4,3,32,128]{3,2,1,0:T(8,128)} %get-tuple-element.18.shard), custom_call_target="tpu_custom_call" | custom-call | tf_op jit(solution)/shard_map/exchange/pallas_call | solution.py:159
  79.8 63.1 %gradient.1 = f32[4,3,512,128]{3,2,1,0:T(8,128)} custom-call(s32[1]{0:T(128)} %get-tuple-element.13.count, s32[17]{0:T(128)} %get-tuple-element.14.slot, s32[17]{0:T(128)} %get-tuple-element.15.row, s32[17]{0:T(128)} %get-tuple-element.16.col, f32[4,3,512,128]{3,2,1,0:T(8,128)} %get-tuple-element.19.field, ...), custom_call_target="tpu_custom_call" | custom-call | tf_op jit(solution)/shard_map/gradient/pallas_call | solution.py:269
  142.9 18.2 %reduce.1 = f32[2,2,32,384]{3,2,1,0:T(8,128)} custom-call(f32[4,3,8,2,32,128]{5,4,3,2,1,0:T(8,128)} %bitcast.1), custom_call_target="tpu_custom_call" | custom-call | tf_op jit(solution)/shard_map/reduce/pallas_call | solution.py:369
  161.1 1.6 copy.11

commit v2 on v1

--- a/solution.py
+++ b/solution.py
@@ -17,7 +17,7 @@
 COL_STEP = 128
 CHIRP = 40.0
 LANES = 128
-CHUNK = 64
+HALF = 64
 VMEM_LIMIT = 60 * 2**20
 
 smem = pl.BlockSpec(memory_space=pltpu.SMEM)
@@ -30,14 +30,33 @@
     angles = ((count[:, None] * count[None, :]) % n).astype(np.float32)
     angles = angles * np.float32(2.0 * math.pi / n)
     scale = np.float32(1.0 / math.sqrt(n))
-    c = np.cos(angles) * scale
-    s = np.sin(angles) * scale
-    forward = np.block([[c, -s], [s, c]]).astype(np.float32)
-    inverse = np.block([[c, s], [-s, c]]).astype(np.float32)
+    c = (np.cos(angles) * scale).astype(np.float32)
+    s = (np.sin(angles) * scale).astype(np.float32)
+    forward = np.block([[c, -s], [s, c]])
+    inverse = np.block([[c, s], [-s, c]])
+    even = np.arange(0, n, 2)
+    odd = even + 1
+    low = np.concatenate([even[: n // 4], odd[: n // 4]])
+
+    def left(sign, inputs):
+        cc = c[np.ix_(low, inputs)]
+        ss = s[np.ix_(low, inputs)] * np.float32(sign)
+        return np.block([[cc, ss], [-ss, cc]])
+
+    left_forward = np.stack([left(1, even), left(1, odd)])
+    left_inverse = np.stack([left(-1, even), left(-1, odd)])
     f = (((count + n // 2) % n) - n // 2).astype(np.float32) / np.float32(n)
     phases = np.float32(CHIRP) * (f[:, None] ** 2 + f[None, :] ** 2)
     kernel = np.stack([np.cos(phases), -np.sin(phases)]).astype(np.float32)
-    return jnp.asarray(forward, bf16), jnp.asarray(inverse, bf16), jnp.asarray(kernel)
+    kernel = kernel[:, np.concatenate([even, odd]), :]
+
+    def low_precision(a):
+        return jnp.asarray(a.astype(np.float32), bf16)
+
+    return (
+        low_precision(forward), low_precision(inverse),
+        low_precision(left_forward), low_precision(left_inverse), jnp.asarray(kernel),
+    )
 
 
 def pack_kernel(tiles, slabs, reads, owner, rowoff, coloff, images, field,
@@ -103,6 +122,12 @@
     )(owner, rowoff, coloff, images, field)
 
 
+ROUTE = (
+    (1, 0), (3, 0), (2, 0), (1, 1), (3, 3), (1, 3), (3, 1), (2, 1),
+    (2, 3), (1, 2), (3, 2), (2, 2), (0, 1), (0, 3), (0, 2),
+)
+
+
 def exchange_kernel(tiles, slabs, rows, packed, shard, got, field,
                     hold, localsem, psend, precv, nsend, nrecv, asend, arecv, bsend, brecv):
     tile = lax.axis_index("tile")
@@ -133,9 +158,10 @@
     ahead = push(shard, after, nsend, nrecv, before, slab)
     for d in range(1, slabs):
         copies.append(push(shard, mine, asend.at[d - 1], arecv.at[d - 1], tile, lax.rem(slab + d, slabs)))
-    for d in range(1, tiles):
-        peer = lax.rem(tile + d, tiles)
-        copies.append(push(packed.at[peer], got.at[tile], psend.at[d - 1], precv.at[d - 1], peer, slab))
+    side = math.isqrt(tiles)
+    for k, (dy, dx) in enumerate(ROUTE):
+        peer = lax.rem(lax.div(tile, side) + dy, side) * side + lax.rem(lax.rem(tile, side) + dx, side)
+        copies.append(push(packed.at[peer], got.at[tile], psend.at[k], precv.at[k], peer, slab))
     keep = pltpu.make_async_copy(shard, mine, localsem.at[0])
     keep.start()
     first = pltpu.make_async_copy(packed.at[tile], hold, localsem.at[1])
@@ -177,111 +203,179 @@
     )(packed, shard)
 
 
-def grad_kernel(count, slot, row, col, field, images, probe, forward, inverse, kernel,
-                total, x, h, y, wave, image, imsem):
-    n = 256
+def product(ar, ai, br, bi):
+    return ar * br - ai * bi, ar * bi + ai * br
+
+
+def conjugate_product(ar, ai, br, bi):
+    return ar * br + ai * bi, ar * bi - ai * br
+
+
+def lanes(c):
+    return slice(c * LANES, (c + 1) * LANES)
+
+
+def rows_of(p, b):
+    return slice(2 * HALF * p + HALF * b, 2 * HALF * p + HALF * b + HALF)
+
+
+def spread_rows(start, p, b):
+    return pl.ds(start + p + 2 * HALF * b, HALF, stride=2)
+
+
+def grad_kernel(count, slot, row, col, field, images, probe_in, rf, ri, lf, li, kernel,
+                total, x, h, y, wave, measured, probe, image, imsem):
+    n = 4 * HALF
+    dump = field.shape[2]
     total[...] = jnp.zeros_like(total)
+    live = count[0]
+    for g in range(4):
+        probe[g] = probe_in[:, lanes(g)]
 
     def fetch(i):
         index = slot[i]
         return pltpu.make_async_copy(
-            images.at[lax.div(index, CAP), lax.rem(index, CAP)], image.at[lax.rem(i, 2)], imsem.at[lax.rem(i, 2)]
+            images.at[lax.div(index, CAP), lax.rem(index, CAP)], image.at[lax.rem(i, 4)], imsem.at[lax.rem(i, 4)]
         )
 
-    def transform(backward):
-        right = inverse if backward else forward
-        left = forward if backward else inverse
-        half = jnp.dot(x[...], right[...], preferred_element_type=f32)
-        h[:n, :] = half[:, :n].astype(bf16)
-        h[n:, :] = half[:, n:].astype(bf16)
-        y[...] = jnp.dot(left[...], h[...], preferred_element_type=f32)
-
-    def product(ar, ai, br, bi):
-        return ar * br - ai * bi, ar * bi + ai * br
-
-    def conjugate_product(ar, ai, br, bi):
-        return ar * br + ai * bi, ar * bi - ai * br
-
-    def step(i, carry):
+    def pattern(i, j, valid):
         top = row[i]
         left = col[i]
-        fetch(i).wait()
-
-        @pl.when(i + 1 < count[0])
+        place = top if valid is None else jnp.where(valid, top, dump)
+        xj, hj, yj, wj, mj = x.at[j], h.at[j], y.at[j], wave.at[j], measured.at[j]
+        source = image.at[lax.rem(i, 4)]
+
+        def window(s, p, b, c):
+            where = spread_rows(top, p, b)
+            return field[2 * s, left + c, where, :], field[2 * s + 1, left + c, where, :]
+
+        def add(s, p, b, c, parts):
+            where = spread_rows(place, p, b)
+            total[2 * s, left + c, where, :] += parts[0]
+            total[2 * s + 1, left + c, where, :] += parts[1]
+
+        def put(p, b, c, parts):
+            xj[rows_of(p, b), lanes(c)] = parts[0].astype(bf16)
+            xj[rows_of(p, b), lanes(2 + c)] = parts[1].astype(bf16)
+
+        def lit(p, b, c):
+            where = spread_rows(0, p, b)
+            return probe[c, where, :], probe[2 + c, where, :]
+
+        def chirp(p, b, c):
+            return kernel[0, rows_of(p, b), lanes(c)], kernel[1, rows_of(p, b), lanes(c)]
+
+        def each(use):
+            for p in range(2):
+                for c in range(2):
+                    l = lanes(c)
+                    parts = [yj[HALF * k:HALF * k + HALF, l] for k in (p, 2 + p, 4 + p, 6 + p)]
+                    use(p, 0, c, parts[0] + parts[2], parts[1] + parts[3])
+                    use(p, 1, c, parts[0] - parts[2], parts[1] - parts[3])
+
+        def transform(backward):
+            right = ri if backward else rf
+            lt = li if backward else lf
+            half = jnp.dot(xj[...], right[...], preferred_element_type=f32)
+            m = n // 2
+            hj[0:m, :] = half[:m, :n].astype(bf16)
+            hj[m:n, :] = half[:m, n:].astype(bf16)
+            hj[n:n + m, :] = half[m:, :n].astype(bf16)
+            hj[n + m:, :] = half[m:, n:].astype(bf16)
+            yj[:n, :] = jnp.dot(lt[0], hj[:n, :], preferred_element_type=f32)
+            yj[n:, :] = jnp.dot(lt[1], hj[n:, :], preferred_element_type=f32)
+
+        def begin():
+            for p in range(2):
+                for b in range(2):
+                    for c in range(2):
+                        put(p, b, c, product(*lit(p, b, c), *window(0, p, b, c)))
+
+        def scatter(p, b, c, re, im):
+            put(p, b, c, product(*chirp(p, b, c), re, im))
+
+        def enter(p, b, c, re, im):
+            wj[rows_of(p, b), lanes(c)] = re
+            wj[rows_of(p, b), lanes(2 + c)] = im
+            put(p, b, c, product(re, im, *window(1, p, b, c)))
+
+        def compare(p, b, c, re, im):
+            misfit = re * re + im * im - mj[c, spread_rows(0, p, b), :]
+            put(p, b, c, (re * misfit, im * misfit))
+
+        def compare_all():
+            for c in range(2):
+                mj[c] = source[:, lanes(c)].astype(f32)
+            each(compare)
+
+        def leave(p, b, c, re, im):
+            add(1, p, b, c, conjugate_product(wj[rows_of(p, b), lanes(c)], wj[rows_of(p, b), lanes(2 + c)], re, im))
+            put(p, b, c, conjugate_product(*window(1, p, b, c), re, im))
+
+        def gather(p, b, c, re, im):
+            put(p, b, c, conjugate_product(*chirp(p, b, c), re, im))
+
+        def finish(p, b, c, re, im):
+            add(0, p, b, c, conjugate_product(*lit(p, b, c), re, im))
+
+        points = [begin, lambda: each(scatter), lambda: each(enter), compare_all,
+                  lambda: each(leave), lambda: each(gather), lambda: each(finish)]
+        return points, transform
+
+    def step(k, carry):
+        a = 2 * k
+        b = jnp.minimum(2 * k + 1, live - 1)
+        valid = 2 * k + 1 < live
+        fetch(a).wait()
+
+        @pl.when(valid)
         def _():
-            fetch(i + 1).start()
-
-        def window(s, q, r, c):
-            return field[2 * s + q, left + c, pl.ds(top + r, CHUNK), :].astype(f32)
-
-        def add(s, r, c, re, im):
-            total[2 * s, left + c, pl.ds(top + r, CHUNK), :] += re
-            total[2 * s + 1, left + c, pl.ds(top + r, CHUNK), :] += im
-
-        def put(r, c, parts):
-            x[r:r + CHUNK, c * LANES:(c + 1) * LANES] = parts[0].astype(bf16)
-            x[r:r + CHUNK, n + c * LANES:n + (c + 1) * LANES] = parts[1].astype(bf16)
-
-        def pieces():
-            for r in range(0, n, CHUNK):
-                for c in range(2):
-                    yield r, c, slice(r, r + CHUNK), slice(n + r, n + r + CHUNK), slice(c * LANES, (c + 1) * LANES)
-
-        for r, c, a, b, l in pieces():
-            put(r, c, product(probe[a, l], probe[a, n + c * LANES:n + (c + 1) * LANES], window(0, 0, r, c), window(0, 1, r, c)))
-        transform(False)
-        for r, c, a, b, l in pieces():
-            put(r, c, product(kernel[0, a, l], kernel[1, a, l], y[a, l], y[b, l]))
-        transform(True)
-        for r, c, a, b, l in pieces():
-            re, im = y[a, l], y[b, l]
-            wave[a, l] = re
-            wave[b, l] = im
-            put(r, c, product(re, im, window(1, 0, r, c), window(1, 1, r, c)))
-        transform(False)
-        for r, c, a, b, l in pieces():
-            re, im = y[a, l], y[b, l]
-            misfit = re * re + im * im - image[lax.rem(i, 2), a, l].astype(f32)
-            put(r, c, (re * misfit, im * misfit))
-        transform(True)
-        for r, c, a, b, l in pieces():
-            re, im = y[a, l], y[b, l]
-            add(1, r, c, *conjugate_product(wave[a, l], wave[b, l], re, im))
-            put(r, c, conjugate_product(window(1, 0, r, c), window(1, 1, r, c), re, im))
-        transform(False)
-        for r, c, a, b, l in pieces():
-            put(r, c, conjugate_product(kernel[0, a, l], kernel[1, a, l], y[a, l], y[b, l]))
-        transform(True)
-        for r, c, a, b, l in pieces():
-            add(0, r, c, *conjugate_product(probe[a, l], probe[a, n + c * LANES:n + (c + 1) * LANES], y[a, l], y[b, l]))
+            fetch(2 * k + 1).wait()
+
+        for ahead in (2, 3):
+            @pl.when(2 * k + ahead < live)
+            def _():
+                fetch(2 * k + ahead).start()
+
+        first, first_transform = pattern(a, 0, None)
+        second, second_transform = pattern(b, 1, valid)
+        first[0]()
+        for t in range(6):
+            first_transform(t % 2 == 1)
+            second[t]()
+            second_transform(t % 2 == 1)
+            first[t + 1]()
+        second[6]()
         return carry
 
-    @pl.when(count[0] > 0)
-    def _():
-        fetch(0).start()
-
-    lax.fori_loop(0, count[0], step, 0)
+    for s in range(2):
+        @pl.when(live > s)
+        def _():
+            fetch(s).start()
+    lax.fori_loop(0, lax.div(live + 1, 2), step, 0)
 
 
 def gradient(count, slot, row, col, field, images, probe):
     n = probe.shape[0]
-    forward, inverse, kernel = make_tables(n)
+    planes, cols, rows, width = field.shape
     return pl.pallas_call(
         grad_kernel,
-        out_shape=jax.ShapeDtypeStruct(field.shape, f32),
-        in_specs=[smem] * 4 + [vmem, anyspace] + [vmem] * 4,
+        out_shape=jax.ShapeDtypeStruct((planes, cols, rows + n, width), f32),
+        in_specs=[smem] * 4 + [vmem, anyspace] + [vmem] * 6,
         out_specs=vmem,
         scratch_shapes=[
-            pltpu.VMEM((n, 2 * n), bf16),
-            pltpu.VMEM((2 * n, n), bf16),
-            pltpu.VMEM((2 * n, n), f32),
-            pltpu.VMEM((2 * n, n), f32),
-            pltpu.VMEM((2, n, n), bf16),
-            pltpu.SemaphoreType.DMA((2,)),
+            pltpu.VMEM((2, n, 2 * n), bf16),
+            pltpu.VMEM((2, 2 * n, n), bf16),
+            pltpu.VMEM((2, 2 * n, n), f32),
+            pltpu.VMEM((2, n, 2 * n), f32),
+            pltpu.VMEM((2, 2, n, width), f32),
+            pltpu.VMEM((4, n, width), f32),
+            pltpu.VMEM((4, n, n), bf16),
+            pltpu.SemaphoreType.DMA((4,)),
         ],
         compiler_params=pltpu.CompilerParams(vmem_limit_bytes=VMEM_LIMIT),
         name="gradient",
-    )(count, slot, row, col, field, images, probe, forward, inverse, kernel)
+    )(count, slot, row, col, field, images, probe, *make_tables(n))
 
 
 def reduce_kernel(tiles, slabs, cores, total, out, part, near, far, outgoing,
@@ -362,10 +456,10 @@
     cores = 2
     levels = slabs // cores
     planes, cols, rows, lanes = total.shape
-    each = rows // (2 * slabs)
+    each = (rows - 256) // (2 * slabs)
     sem = pltpu.SemaphoreType.DMA
-    total = total.reshape(planes, cols, 2 * levels, cores, each, lanes)
     count = 2 * levels
+    total = total.reshape(planes, cols, rows // (cores * each), cores, each, lanes)
     return pl.pallas_call(
         functools.partial(reduce_kernel, tiles, slabs, cores),
         out_shape=jax.ShapeDtypeStruct((2, 2, each, cols * lanes), f32),

time: 165 us -> 145 us (0.88)
  the two profiles are of different devices: /device:TPU:1 before, /device:TPU:19 now
where the time goes in v2:
time: 145 us
  Pallas kernels  143 us (99%)
  local copies, waits for them, and re-layouts  1.62 us (1%)
    pallas_call x1, Pallas kernels, exchange(): pl.pallas_call(functools.partial(exchange_kernel, tiles, slabs, rows), ou...  75.3 us
    pallas_call x1, Pallas kernels, gradient(): pl.pallas_call(grad_kernel, out_shape=jax.ShapeDtypeStruct((planes, cols,...  46.6 us
    pallas_call x1, Pallas kernels, reduce(): pl.pallas_call(functools.partial(reduce_kernel, tiles, slabs, cores), out...  16.5 us
    pallas_call x1, Pallas kernels, pack(): pl.pallas_call(functools.partial(pack_kernel, tiles, slabs, reads), out_s...  4.63 us

profile of v2, /device:TPU:19, one launch (start us, length us, event | category | flops | bytes accessed | tf_op | source)
XLA Modules:
  0.0 144.6 jit_solution(5594037176050850781)
XLA Ops:
  0.0 4.6 %pack.1 = (bf16[16,2,256,256]{3,2,1,0:T(8,128)(2,1)}, s32[1]{0:T(128)}, s32[17]{0:T(128)}, s32[17]{0:T(128)}, s32[17]{0:T(128)}, /*index=5*/f32[4,3,32,128]{3,2,1,0:T(8,128)}) custom-call(s32[1792]{0:T(1024)} %owner.1, s32[1792]{0:T(1024)} %rowoff.1, s32[1792]{0:T(1024)} %coloff.1, bf16[14,256,256]{2,1,0:T(8,128)(2,1)} %images.1, f32[2,2,32,384]{3,2,1,0:T(8,128)} %field.1), custom_call_target="tpu_custom_call" | custom-call | tf_op jit(solution)/shard_map/pack/pallas_call | solution.py:103
  4.6 75.3 %exchange.1 = (bf16[16,2,256,256]{3,2,1,0:T(8,128)(2,1)}, f32[4,3,512,128]{3,2,1,0:T(8,128)}) custom-call(bf16[16,2,256,256]{3,2,1,0:T(8,128)(2,1)} %get-tuple-element.17.packed, f32[4,3,32,128]{3,2,1,0:T(8,128)} %get-tuple-element.18.shard), custom_call_target="tpu_custom_call" | custom-call | tf_op jit(solution)/shard_map/exchange/pallas_call | solution.py:185
  79.9 46.6 %gradient.1 = f32[4,3,768,128]{3,2,1,0:T(8,128)} custom-call(s32[1]{0:T(128)} %get-tuple-element.13.count, s32[17]{0:T(128)} %get-tuple-element.14.slot, s32[17]{0:T(128)} %get-tuple-element.15.row, s32[17]{0:T(128)} %get-tuple-element.16.col, f32[4,3,512,128]{3,2,1,0:T(8,128)} %get-tuple-element.19.field, ...), custom_call_target="tpu_custom_call" | custom-call | tf_op jit(solution)/shard_map/gradient/pallas_call | solution.py:361
  126.5 16.5 %reduce.1 = f32[2,2,32,384]{3,2,1,0:T(8,128)} custom-call(f32[4,3,12,2,32,128]{5,4,3,2,1,0:T(8,128)} %bitcast.1), custom_call_target="tpu_custom_call" | custom-call | tf_op jit(solution)/shard_map/reduce/pallas_call | solution.py:463
  143.0 1.6 %copy.13 = f32[2,2,32,384]{3,2,1,0:T(8,128)} copy(f32[2,2,32,384]{3,2,1,0:T(8,128)} %reduce.1) | data formatting | bytes 393216

commit v3 on v2

--- a/solution.py
+++ b/solution.py
@@ -67,6 +67,10 @@
         pltpu.make_async_copy(images.at[k], hold.at[k], insem.at[k]).start()
     for t in range(tiles):
         used[t] = 0
+    for k in range(K + 1):
+        slot[k] = 0
+        row[k] = 0
+        col[k] = 0
     for k in range(reads):
         dest = owner[(tile * slabs + slab) * reads + k]
         rank = used[dest]
@@ -84,7 +88,7 @@
         def one(k, state):
             n, rank = state
             hit = owner[base + k] == tile
-            slot[n] = i * CAP + rank
+            slot[n] = jnp.where(hit, i * CAP + rank, 0)
             row[n] = rowoff[base + k]
             col[n] = coloff[base + k]
             step = hit.astype(jnp.int32)
@@ -122,260 +126,403 @@
     )(owner, rowoff, coloff, images, field)
 
 
-ROUTE = (
-    (1, 0), (3, 0), (2, 0), (1, 1), (3, 3), (1, 3), (3, 1), (2, 1),
-    (2, 3), (1, 2), (3, 2), (2, 2), (0, 1), (0, 3), (0, 2),
-)
-
-
-def exchange_kernel(tiles, slabs, rows, packed, shard, got, field,
-                    hold, localsem, psend, precv, nsend, nrecv, asend, arecv, bsend, brecv):
+def product(ar, ai, br, bi):
+    return ar * br - ai * bi, ar * bi + ai * br
+
+
+def conjugate_product(ar, ai, br, bi):
+    return ar * br + ai * bi, ar * bi - ai * br
+
+
+def lanes(c):
+    return slice(c * LANES, (c + 1) * LANES)
+
+
+def rows_of(p, b):
+    return slice(2 * HALF * p + HALF * b, 2 * HALF * p + HALF * b + HALF)
+
+
+def spread_rows(start, p, b):
+    return pl.ds(start + p + 2 * HALF * b, HALF, stride=2)
+
+
+def window(field, s, top, left, p, b, c):
+    where = spread_rows(top, p, b)
+    return field[2 * s, left + c, where, :], field[2 * s + 1, left + c, where, :]
+
+
+def put(x, p, b, c, parts):
+    x[rows_of(p, b), lanes(c)] = parts[0].astype(bf16)
+    x[rows_of(p, b), lanes(2 + c)] = parts[1].astype(bf16)
+
+
+def chirp(kernel, p, b, c):
+    return kernel[0, rows_of(p, b), lanes(c)], kernel[1, rows_of(p, b), lanes(c)]
+
+
+def lit(probe, p, b, c):
+    where = spread_rows(0, p, b)
+    return probe[c, where, :], probe[2 + c, where, :]
+
+
+def each(y, use):
+    for p in range(2):
+        for c in range(2):
+            parts = [y[HALF * k:HALF * k + HALF, lanes(c)] for k in (p, 2 + p, 4 + p, 6 + p)]
+            use(p, 0, c, parts[0] + parts[2], parts[1] + parts[3])
+            use(p, 1, c, parts[0] - parts[2], parts[1] - parts[3])
+
+
+def transform(x, h, y, right, left):
+    n = 4 * HALF
+    m = n // 2
+    half = jnp.dot(x[...], right[...], preferred_element_type=f32)
+    h[0:m, :] = half[:m, :n].astype(bf16)
+    h[m:n, :] = half[:m, n:].astype(bf16)
+    h[n:n + m, :] = half[m:, :n].astype(bf16)
+    h[n + m:, :] = half[m:, n:].astype(bf16)
+    y[:n, :] = jnp.dot(left[0], h[:n, :], preferred_element_type=f32)
+    y[n:, :] = jnp.dot(left[1], h[n:, :], preferred_element_type=f32)
+
+
+def interleave(first, second, transforms):
+    first[0]()
+    for t in range(transforms):
+        first[2 * t + 1]()
+        second[2 * t]()
+        second[2 * t + 1]()
+        first[2 * t + 2]()
+    second[2 * transforms]()
+
+
+XORDER = (1, 3, 2)
+RELAY_STEPS = ((1, slice(3, 6)), (5, slice(6, 9)))
+YORDER = (2, 1, 3)
+
+
+def exchange_kernel(tiles, slabs, cores, rows, packed, shard, slot, row, col, probe_in, rf, ri, lf, li, kernel,
+                    got, field_out, fars, waves,
+                    field, probe, x, h, y, far, wave, hold, localsem, outsem,
+                    stage, xsend, xrecv, ysend, yrecv, nsend, nrecv, zsend, zrecv, csend, crecv):
     tile = lax.axis_index("tile")
     slab = lax.axis_index("slab")
+    levels = slabs // cores
+    core = lax.rem(slab, cores)
+    level = lax.div(slab, cores)
+    other = level * cores + (1 - core)
     before = lax.rem(tile + tiles - 1, tiles)
+    side = math.isqrt(tiles)
     barrier = pltpu.get_barrier_semaphore()
+
+    def greet(t, s):
+        pl.semaphore_signal(barrier, inc=1, device_id={"tile": t, "slab": s}, device_id_type=MESH)
+
     for d in range(1, tiles):
-        peer = lax.rem(tile + d, tiles)
-        pl.semaphore_signal(barrier, inc=1, device_id={"tile": peer, "slab": slab}, device_id_type=MESH)
-    for d in range(1, slabs):
-        peer = lax.rem(slab + d, slabs)
-        pl.semaphore_signal(barrier, inc=1, device_id={"tile": tile, "slab": peer}, device_id_type=MESH)
-    pl.semaphore_wait(barrier, tiles - 1 + slabs - 1)
+        greet(lax.rem(tile + d, tiles), slab)
+    for d in range(1, levels):
+        greet(tile, lax.rem(level + d, levels) * cores + core)
+    greet(tile, other)
+    pl.semaphore_wait(barrier, tiles + levels - 1)
 
     height = rows * slabs
-    mine = field.at[:, :, pl.ds(pl.multiple_of(slab * rows, rows), rows), :]
-    after = field.at[:, :, pl.ds(pl.multiple_of(height + slab * rows, rows), rows), :]
+
+    def block(which, s):
+        return field.at[:, :, pl.ds(pl.multiple_of(which * height + s * rows, rows), rows), :]
+
     copies = []
-
-    def push(src, dst, send, recv, t, s):
+    rims = []
+
+    def make(src, dst, send, recv, t, s):
         copy = pltpu.make_async_remote_copy(
             src_ref=src, dst_ref=dst, send_sem=send, recv_sem=recv,
             device_id={"tile": t, "slab": s}, device_id_type=MESH,
         )
+        copies.append(copy)
+        return copy
+
+    def push(*parts):
+        copy = make(*parts)
         copy.start()
         return copy
 
-    ahead = push(shard, after, nsend, nrecv, before, slab)
-    for d in range(1, slabs):
-        copies.append(push(shard, mine, asend.at[d - 1], arecv.at[d - 1], tile, lax.rem(slab + d, slabs)))
-    side = math.isqrt(tiles)
-    for k, (dy, dx) in enumerate(ROUTE):
-        peer = lax.rem(lax.div(tile, side) + dy, side) * side + lax.rem(lax.rem(tile, side) + dx, side)
-        copies.append(push(packed.at[peer], got.at[tile], psend.at[k], precv.at[k], peer, slab))
-    keep = pltpu.make_async_copy(shard, mine, localsem.at[0])
+    def share(which, src, k):
+        mine = block(which, slab)
+        links = []
+        for d in (2, 1, 3)[: levels - 1]:
+            place = lax.rem(level + d, levels) * cores + core
+            links.append((d, push(src, mine, zsend.at[which, d - 1], zrecv.at[which, d - 1], tile, place)))
+        rims.append(push(src, mine, csend.at[which, 0], crecv.at[which, 0], tile, other))
+        return links
+
+    def pass_on(which, links):
+        for d, copy in links:
+            copy.wait_recv()
+            s = lax.rem(level + levels - d, levels) * cores + core
+            rims.append(push(block(which, s), block(which, s), csend.at[which, d], crecv.at[which, d], tile, other))
+
+    ahead = push(shard, block(1, slab), nsend, nrecv, before, slab)
+    own = share(0, shard, 0)
+    grid_row, grid_col = lax.div(tile, side), lax.rem(tile, side)
+
+    def at(dy, dx):
+        return lax.rem(grid_row + dy + side, side) * side + lax.rem(grid_col + dx + side, side)
+
+    steps = XORDER
+    for dy in YORDER:
+        push(packed.at[at(dy, 0)], got.at[tile], ysend.at[0, dy - 1], yrecv.at[0, dy - 1], at(dy, 0), slab)
+    relays = []
+    for dy in YORDER:
+        for dx in steps:
+            copy = push(packed.at[at(dy, dx)], stage.at[dy - 1, dx - 1], xsend.at[dy, dx - 1], xrecv.at[dy, dx - 1], at(0, dx), slab)
+            relays.append((dy, dx, copy))
+    for dx in steps:
+        push(packed.at[at(0, dx)], got.at[tile], xsend.at[0, dx - 1], xrecv.at[0, dx - 1], at(0, dx), slab)
+    keep = pltpu.make_async_copy(shard, block(0, slab), localsem.at[0])
     keep.start()
     first = pltpu.make_async_copy(packed.at[tile], hold, localsem.at[1])
     first.start()
     first.wait()
     second = pltpu.make_async_copy(hold, got.at[tile], localsem.at[1])
     second.start()
-    ahead.wait()
-    for d in range(1, slabs):
-        copies.append(push(after, after, bsend.at[d - 1], brecv.at[d - 1], tile, lax.rem(slab + d, slabs)))
+    ahead.wait_recv()
+    following = share(1, block(1, slab), 1)
+    def relay(part):
+        for (dy, dx, copy), onward in part:
+            copy.wait_recv()
+            onward.start()
+
+    onwards = [
+        make(stage.at[dy - 1, dx - 1], got.at[at(0, -dx)], ysend.at[dx, dy - 1], yrecv.at[dx, dy - 1], at(dy, 0), slab)
+        for dy, dx, _ in relays
+    ]
+    relays = list(zip(relays, onwards))
+
+    for g in range(4):
+        probe[g] = probe_in[:, lanes(g)]
+    pass_on(0, own)
+    relay(relays[:3])
+    pass_on(1, following)
+    done = [id(c) for _, c in own + following] + [id(ahead)] + [id(r[2]) for r, _ in relays]
+    for copy in rims:
+        copy.wait_recv()
+        done.append(id(copy))
+    keep.wait()
+    store = pltpu.make_async_copy(field, field_out, localsem.at[0])
+    store.start()
+
+    def outputs(k, j):
+        turn = lax.rem(k, 2)
+        return (
+            pltpu.make_async_copy(far.at[turn, j], fars.at[2 * k + j], outsem.at[turn, j, 0]),
+            pltpu.make_async_copy(wave.at[turn, j], waves.at[2 * k + j], outsem.at[turn, j, 1]),
+        )
+
+    def pattern(k, j):
+        top = row[2 * k + j]
+        left = col[2 * k + j]
+        turn = lax.rem(k, 2)
+        xj, hj, yj, fj, wj = x.at[j], h.at[j], y.at[j], far.at[turn, j], wave.at[turn, j]
+
+        def begin():
+            for p in range(2):
+                for b in range(2):
+                    for c in range(2):
+                        put(xj, p, b, c, product(*lit(probe, p, b, c), *window(field, 0, top, left, p, b, c)))
+
+        def scatter(p, b, c, re, im):
+            put(xj, p, b, c, product(*chirp(kernel, p, b, c), re, im))
+
+        def enter(p, b, c, re, im):
+            wj[rows_of(p, b), lanes(c)] = re
+            wj[rows_of(p, b), lanes(2 + c)] = im
+            put(xj, p, b, c, product(re, im, *window(field, 1, top, left, p, b, c)))
+
+        return [
+            begin, lambda: transform(xj, hj, yj, rf, lf), lambda: each(yj, scatter),
+            lambda: transform(xj, hj, yj, ri, li), lambda: each(yj, enter),
+            lambda: transform(xj, hj, fj, rf, lf), lambda: None,
+        ]
+
+    def step(k, carry):
+        @pl.when(k >= 2)
+        def _():
+            for j in range(2):
+                for copy in outputs(k - 2, j):
+                    copy.wait()
+
+        interleave(pattern(k, 0), pattern(k, 1), 3)
+        for j in range(2):
+            for copy in outputs(k, j):
+                copy.start()
+
+        for when, part in RELAY_STEPS:
+            @pl.when(k == when)
+            def _():
+                relay(relays[part])
+
+        return carry
+
+    pairs = K // 2
+    lax.fori_loop(0, pairs, step, 0)
+    for k in (pairs - 2, pairs - 1):
+        for j in range(2):
+            for copy in outputs(k, j):
+                copy.wait()
+    store.wait()
     second.wait()
-    keep.wait()
     for copy in copies:
-        copy.wait()
-
-
-def exchange(packed, shard, tiles, slabs):
+        copy.wait_send()
+        if id(copy) not in done:
+            copy.wait_recv()
+
+
+def exchange(packed, shard, slot, row, col, probe, tables, tiles, slabs):
     _, _, n, _ = packed.shape
-    planes, cols, rows, lanes = shard.shape
+    planes, cols, rows, width = shard.shape
+    cores = 2
+    levels = slabs // cores
+    side = math.isqrt(tiles)
     sem = pltpu.SemaphoreType.DMA
+    extended = (planes, cols, 2 * rows * slabs, width)
     return pl.pallas_call(
-        functools.partial(exchange_kernel, tiles, slabs, rows),
+        functools.partial(exchange_kernel, tiles, slabs, cores, rows),
         out_shape=(
             jax.ShapeDtypeStruct(packed.shape, packed.dtype),
-            jax.ShapeDtypeStruct((planes, cols, 2 * rows * slabs, lanes), shard.dtype),
+            jax.ShapeDtypeStruct(extended, f32),
+            jax.ShapeDtypeStruct((K, 2 * n, n), f32),
+            jax.ShapeDtypeStruct((K, n, 2 * n), f32),
         ),
-        in_specs=[anyspace, vmem],
-        out_specs=(anyspace, anyspace),
+        in_specs=[anyspace, vmem, smem, smem, smem] + [vmem] * 6,
+        out_specs=(anyspace,) * 4,
         scratch_shapes=[
+            pltpu.VMEM(extended, f32),
+            pltpu.VMEM((4, n, width), f32),
+            pltpu.VMEM((2, n, 2 * n), bf16),
+            pltpu.VMEM((2, 2 * n, n), bf16),
+            pltpu.VMEM((2, 2 * n, n), f32),
+            pltpu.VMEM((2, 2, 2 * n, n), f32),
+            pltpu.VMEM((2, 2, n, 2 * n), f32),
             pltpu.VMEM((CAP, n, n), bf16),
             sem((2,)),
-            sem((tiles - 1,)), sem((tiles - 1,)),
+            sem((2, 2, 2)),
+            pltpu.VMEM((side - 1, side - 1, CAP, n, n), bf16),
+            sem((side, side - 1)), sem((side, side - 1)),
+            sem((side, side - 1)), sem((side, side - 1)),
             sem, sem,
-            sem((slabs - 1,)), sem((slabs - 1,)),
-            sem((slabs - 1,)), sem((slabs - 1,)),
+            sem((2, levels - 1)), sem((2, levels - 1)),
+            sem((2, levels)), sem((2, levels)),
         ],
-        compiler_params=pltpu.CompilerParams(collective_id=0, has_side_effects=True),
+        compiler_params=pltpu.CompilerParams(collective_id=0, has_side_effects=True, vmem_limit_bytes=VMEM_LIMIT),
         name="exchange",
-    )(packed, shard)
-
-
-def product(ar, ai, br, bi):
-    return ar * br - ai * bi, ar * bi + ai * br
-
-
-def conjugate_product(ar, ai, br, bi):
-    return ar * br + ai * bi, ar * bi - ai * br
-
-
-def lanes(c):
-    return slice(c * LANES, (c + 1) * LANES)
-
-
-def rows_of(p, b):
-    return slice(2 * HALF * p + HALF * b, 2 * HALF * p + HALF * b + HALF)
-
-
-def spread_rows(start, p, b):
-    return pl.ds(start + p + 2 * HALF * b, HALF, stride=2)
-
-
-def grad_kernel(count, slot, row, col, field, images, probe_in, rf, ri, lf, li, kernel,
-                total, x, h, y, wave, measured, probe, image, imsem):
-    n = 4 * HALF
+    )(packed, shard, slot, row, col, probe, *tables)
+
+
+def grad_kernel(count, slot, row, col, field, images, fars, waves, probe_in, rf, ri, lf, li, kernel,
+                total, x, h, y, far, wave, measured, probe, image, insem):
     dump = field.shape[2]
     total[...] = jnp.zeros_like(total)
     live = count[0]
     for g in range(4):
         probe[g] = probe_in[:, lanes(g)]
 
-    def fetch(i):
+    def inputs(i):
         index = slot[i]
-        return pltpu.make_async_copy(
-            images.at[lax.div(index, CAP), lax.rem(index, CAP)], image.at[lax.rem(i, 4)], imsem.at[lax.rem(i, 4)]
+        place = lax.rem(i, 4)
+        return (
+            pltpu.make_async_copy(images.at[lax.div(index, CAP), lax.rem(index, CAP)], image.at[place], insem.at[place, 0]),
+            pltpu.make_async_copy(fars.at[i], far.at[place], insem.at[place, 1]),
+            pltpu.make_async_copy(waves.at[i], wave.at[place], insem.at[place, 2]),
         )
 
     def pattern(i, j, valid):
         top = row[i]
         left = col[i]
         place = top if valid is None else jnp.where(valid, top, dump)
-        xj, hj, yj, wj, mj = x.at[j], h.at[j], y.at[j], wave.at[j], measured.at[j]
-        source = image.at[lax.rem(i, 4)]
-
-        def window(s, p, b, c):
-            where = spread_rows(top, p, b)
-            return field[2 * s, left + c, where, :], field[2 * s + 1, left + c, where, :]
+        at = lax.rem(i, 4)
+        xj, hj, yj, mj = x.at[j], h.at[j], y.at[j], measured.at[j]
+        wj, fj, source = wave.at[at], far.at[at], image.at[at]
 
         def add(s, p, b, c, parts):
             where = spread_rows(place, p, b)
             total[2 * s, left + c, where, :] += parts[0]
             total[2 * s + 1, left + c, where, :] += parts[1]
 
-        def put(p, b, c, parts):
-            xj[rows_of(p, b), lanes(c)] = parts[0].astype(bf16)
-            xj[rows_of(p, b), lanes(2 + c)] = parts[1].astype(bf16)
-
-        def lit(p, b, c):
-            where = spread_rows(0, p, b)
-            return probe[c, where, :], probe[2 + c, where, :]
-
-        def chirp(p, b, c):
-            return kernel[0, rows_of(p, b), lanes(c)], kernel[1, rows_of(p, b), lanes(c)]
-
-        def each(use):
-            for p in range(2):
-                for c in range(2):
-                    l = lanes(c)
-                    parts = [yj[HALF * k:HALF * k + HALF, l] for k in (p, 2 + p, 4 + p, 6 + p)]
-                    use(p, 0, c, parts[0] + parts[2], parts[1] + parts[3])
-                    use(p, 1, c, parts[0] - parts[2], parts[1] - parts[3])
-
-        def transform(backward):
-            right = ri if backward else rf
-            lt = li if backward else lf
-            half = jnp.dot(xj[...], right[...], preferred_element_type=f32)
-            m = n // 2
-            hj[0:m, :] = half[:m, :n].astype(bf16)
-            hj[m:n, :] = half[:m, n:].astype(bf16)
-            hj[n:n + m, :] = half[m:, :n].astype(bf16)
-            hj[n + m:, :] = half[m:, n:].astype(bf16)
-            yj[:n, :] = jnp.dot(lt[0], hj[:n, :], preferred_element_type=f32)
-            yj[n:, :] = jnp.dot(lt[1], hj[n:, :], preferred_element_type=f32)
-
-        def begin():
-            for p in range(2):
-                for b in range(2):
-                    for c in range(2):
-                        put(p, b, c, product(*lit(p, b, c), *window(0, p, b, c)))
-
-        def scatter(p, b, c, re, im):
-            put(p, b, c, product(*chirp(p, b, c), re, im))
-
-        def enter(p, b, c, re, im):
-            wj[rows_of(p, b), lanes(c)] = re
-            wj[rows_of(p, b), lanes(2 + c)] = im
-            put(p, b, c, product(re, im, *window(1, p, b, c)))
-
         def compare(p, b, c, re, im):
             misfit = re * re + im * im - mj[c, spread_rows(0, p, b), :]
-            put(p, b, c, (re * misfit, im * misfit))
+            put(xj, p, b, c, (re * misfit, im * misfit))
 
         def compare_all():
             for c in range(2):
                 mj[c] = source[:, lanes(c)].astype(f32)
-            each(compare)
+            each(fj, compare)
 
         def leave(p, b, c, re, im):
             add(1, p, b, c, conjugate_product(wj[rows_of(p, b), lanes(c)], wj[rows_of(p, b), lanes(2 + c)], re, im))
-            put(p, b, c, conjugate_product(*window(1, p, b, c), re, im))
+            put(xj, p, b, c, conjugate_product(*window(field, 1, top, left, p, b, c), re, im))
 
         def gather(p, b, c, re, im):
-            put(p, b, c, conjugate_product(*chirp(p, b, c), re, im))
+            put(xj, p, b, c, conjugate_product(*chirp(kernel, p, b, c), re, im))
 
         def finish(p, b, c, re, im):
-            add(0, p, b, c, conjugate_product(*lit(p, b, c), re, im))
-
-        points = [begin, lambda: each(scatter), lambda: each(enter), compare_all,
-                  lambda: each(leave), lambda: each(gather), lambda: each(finish)]
-        return points, transform
+            add(0, p, b, c, conjugate_product(*lit(probe, p, b, c), re, im))
+
+        return [
+            compare_all, lambda: transform(xj, hj, yj, ri, li), lambda: each(yj, leave),
+            lambda: transform(xj, hj, yj, rf, lf), lambda: each(yj, gather),
+            lambda: transform(xj, hj, yj, ri, li), lambda: each(yj, finish),
+        ]
 
     def step(k, carry):
         a = 2 * k
         b = jnp.minimum(2 * k + 1, live - 1)
         valid = 2 * k + 1 < live
-        fetch(a).wait()
+        for copy in inputs(a):
+            copy.wait()
 
         @pl.when(valid)
         def _():
-            fetch(2 * k + 1).wait()
+            for copy in inputs(2 * k + 1):
+                copy.wait()
 
         for ahead in (2, 3):
             @pl.when(2 * k + ahead < live)
             def _():
-                fetch(2 * k + ahead).start()
-
-        first, first_transform = pattern(a, 0, None)
-        second, second_transform = pattern(b, 1, valid)
-        first[0]()
-        for t in range(6):
-            first_transform(t % 2 == 1)
-            second[t]()
-            second_transform(t % 2 == 1)
-            first[t + 1]()
-        second[6]()
+                for copy in inputs(2 * k + ahead):
+                    copy.start()
+
+        interleave(pattern(a, 0, None), pattern(b, 1, valid), 3)
         return carry
 
     for s in range(2):
         @pl.when(live > s)
         def _():
-            fetch(s).start()
+            for copy in inputs(s):
+                copy.start()
     lax.fori_loop(0, lax.div(live + 1, 2), step, 0)
 
 
-def gradient(count, slot, row, col, field, images, probe):
+def gradient(count, slot, row, col, field, images, fars, waves, probe, tables):
     n = probe.shape[0]
     planes, cols, rows, width = field.shape
     return pl.pallas_call(
         grad_kernel,
         out_shape=jax.ShapeDtypeStruct((planes, cols, rows + n, width), f32),
-        in_specs=[smem] * 4 + [vmem, anyspace] + [vmem] * 6,
+        in_specs=[smem] * 4 + [vmem] + [anyspace] * 3 + [vmem] * 6,
         out_specs=vmem,
         scratch_shapes=[
             pltpu.VMEM((2, n, 2 * n), bf16),
             pltpu.VMEM((2, 2 * n, n), bf16),
             pltpu.VMEM((2, 2 * n, n), f32),
-            pltpu.VMEM((2, n, 2 * n), f32),
+            pltpu.VMEM((4, 2 * n, n), f32),
+            pltpu.VMEM((4, n, 2 * n), f32),
             pltpu.VMEM((2, 2, n, width), f32),
             pltpu.VMEM((4, n, width), f32),
             pltpu.VMEM((4, n, n), bf16),
-            pltpu.SemaphoreType.DMA((4,)),
+            pltpu.SemaphoreType.DMA((4, 3)),
         ],
         compiler_params=pltpu.CompilerParams(vmem_limit_bytes=VMEM_LIMIT),
         name="gradient",
-    )(count, slot, row, col, field, images, probe, *make_tables(n))
+    )(count, slot, row, col, field, images, fars, waves, probe, *tables)
 
 
 def reduce_kernel(tiles, slabs, cores, total, out, part, near, far, outgoing,
@@ -486,8 +633,9 @@
     packed, count, slot, row, col, shard = pack(
         owner_tile, row_offset, col_offset, intensities, object_field, tiles, slabs
     )
-    images, field = exchange(packed, shard, tiles, slabs)
-    total = gradient(count, slot, row, col, field, images, probe_wave)
+    tables = make_tables(intensities.shape[1])
+    images, field, fars, waves = exchange(packed, shard, slot, row, col, probe_wave, tables, tiles, slabs)
+    total = gradient(count, slot, row, col, field, images, fars, waves, probe_wave, tables)
     return reduce(total, tiles, slabs)
 
 

time: 145 us -> 123 us (0.85)
  the two profiles are of different devices: /device:TPU:19 before, /device:TPU:1 now
where the time goes in v3:
time: 123 us; the launch traced here: 122 us
  Pallas kernels  121 us (98%)
  local copies, waits for them, and re-layouts  1.62 us (1%)
    pallas_call x1, Pallas kernels, exchange(): pl.pallas_call(functools.partial(exchange_kernel, tiles, slabs, cores, ro...  65.8 us
    pallas_call x1, Pallas kernels, gradient(): pl.pallas_call(grad_kernel, out_shape=jax.ShapeDtypeStruct((planes, cols,...  27.2 us
    pallas_call x1, Pallas kernels, reduce(): pl.pallas_call(functools.partial(reduce_kernel, tiles, slabs, cores), out...  23.1 us
    pallas_call x1, Pallas kernels, pack(): pl.pallas_call(functools.partial(pack_kernel, tiles, slabs, reads), out_s...  4.69 us

profile of v3, /device:TPU:1, one launch (start us, length us, event | category | flops | bytes accessed | tf_op | source)
XLA Modules:
  0.0 122.4 jit_solution(14725423697219051192)
XLA Ops:
  0.0 4.7 %pack.1 = (bf16[16,2,256,256]{3,2,1,0:T(8,128)(2,1)}, s32[1]{0:T(128)}, s32[17]{0:T(128)}, s32[17]{0:T(128)}, s32[17]{0:T(128)}, /*index=5*/f32[4,3,32,128]{3,2,1,0:T(8,128)}) custom-call(s32[1792]{0:T(1024)} %owner.1, s32[1792]{0:T(1024)} %rowoff.1, s32[1792]{0:T(1024)} %coloff.1, bf16[14,256,256]{2,1,0:T(8,128)(2,1)} %images.1, f32[2,2,32,384]{3,2,1,0:T(8,128)} %field.1), custom_call_target="tpu_custom_call" | custom-call | tf_op jit(solution)/shard_map/pack/pallas_call | solution.py:107
  4.7 65.8 %exchange.1 = (bf16[16,2,256,256]{3,2,1,0:T(8,128)(2,1)}, f32[4,3,512,128]{3,2,1,0:T(8,128)}, f32[16,512,256]{2,1,0:T(8,128)}, f32[16,256,512]{2,1,0:T(8,128)}) custom-call(bf16[16,2,256,256]{3,2,1,0:T(8,128)(2,1)} %get-tuple-element.19.packed, f32[4,3,32,128]{3,2,1,0:T(8,128)} %get-tuple-element.20.shard, s32[17]{0:T(128)} %get-tuple-element.16.slot, ...), custom_call_target="tpu_custom_call" | custom-call | tf_op jit(solution)/shard_map/exchange/pallas_call | solution.py:387
  70.5 27.2 %gradient.1 = f32[4,3,768,128]{3,2,1,0:T(8,128)} custom-call(s32[1]{0:T(128)} %get-tuple-element.15.count, s32[17]{0:T(128)} %get-tuple-element.16.slot, s32[17]{0:T(128)} %get-tuple-element.17.row, s32[17]{0:T(128)} %get-tuple-element.18.col, f32[4,3,512,128]{3,2,1,0:T(8,128)} %get-tuple-element.21.field, ...), custom_call_target="tpu_custom_call" | custom-call | tf_op jit(solution)/shard_map/gradient/pallas_call | solution.py:507
  97.7 23.1 %reduce.1 = f32[2,2,32,384]{3,2,1,0:T(8,128)} custom-call(f32[4,3,12,2,32,128]{5,4,3,2,1,0:T(8,128)} %bitcast.1), custom_call_target="tpu_custom_call" | custom-call | tf_op jit(solution)/shard_map/reduce/pallas_call | solution.py:610
  120.8 1.6 %copy.13 = f32[2,2,32,384]{3,2,1,0:T(8,128)} copy(f32[2,2,32,384]{3,2,1,0:T(8,128)} %reduce.1) | data formatting | bytes 393216

commit v4 on v3

--- a/solution.py
+++ b/solution.py
@@ -18,6 +18,7 @@
 CHIRP = 40.0
 LANES = 128
 HALF = 64
+CHUNK = 32
 VMEM_LIMIT = 60 * 2**20
 
 smem = pl.BlockSpec(memory_space=pltpu.SMEM)
@@ -32,35 +33,56 @@
     scale = np.float32(1.0 / math.sqrt(n))
     c = (np.cos(angles) * scale).astype(np.float32)
     s = (np.sin(angles) * scale).astype(np.float32)
-    forward = np.block([[c, -s], [s, c]])
-    inverse = np.block([[c, s], [-s, c]])
     even = np.arange(0, n, 2)
     odd = even + 1
     low = np.concatenate([even[: n // 4], odd[: n // 4]])
+    near = np.arange(n // 2)
 
     def left(sign, inputs):
         cc = c[np.ix_(low, inputs)]
         ss = s[np.ix_(low, inputs)] * np.float32(sign)
         return np.block([[cc, ss], [-ss, cc]])
 
-    left_forward = np.stack([left(1, even), left(1, odd)])
-    left_inverse = np.stack([left(-1, even), left(-1, odd)])
+    def right(sign, inputs, outputs):
+        cc = c[np.ix_(inputs, outputs)]
+        ss = s[np.ix_(inputs, outputs)] * np.float32(sign)
+        return np.block([[cc, -ss], [ss, cc]])
+
     f = (((count + n // 2) % n) - n // 2).astype(np.float32) / np.float32(n)
     phases = np.float32(CHIRP) * (f[:, None] ** 2 + f[None, :] ** 2)
     kernel = np.stack([np.cos(phases), -np.sin(phases)]).astype(np.float32)
-    kernel = kernel[:, np.concatenate([even, odd]), :]
+    kernel = kernel[:, np.concatenate([even, odd]), :][:, :, np.concatenate([low, low + n // 2])]
 
     def low_precision(a):
         return jnp.asarray(a.astype(np.float32), bf16)
 
-    return (
-        low_precision(forward), low_precision(inverse),
-        low_precision(left_forward), low_precision(left_inverse), jnp.asarray(kernel),
+    return dict(
+        left_forward=low_precision(np.stack([left(1, even), left(1, odd)])),
+        left_inverse=low_precision(np.stack([left(-1, even), left(-1, odd)])),
+        right_forward=low_precision(np.stack([right(1, even, low), right(1, odd, low)])),
+        right_inverse=low_precision(np.stack([right(-1, even, low), right(-1, odd, low)])),
+        right_far=low_precision(np.stack([right(1, even, near), right(1, odd, near)])),
+        right_back=low_precision(np.concatenate([right(-1, count, low), right(-1, count, low + n // 2)], 1)),
+        kernel=jnp.asarray(kernel),
     )
 
 
-def pack_kernel(tiles, slabs, reads, owner, rowoff, coloff, images, field,
-                packed, count, slot, row, col, shard, hold, used, insem, outsem):
+def lane_order():
+    order = np.concatenate([np.arange(0, LANES, 2), np.arange(1, LANES, 2)])
+    return jnp.asarray(order[None, :] == np.arange(LANES)[:, None], bf16)
+
+
+def rearrange(value, order):
+    high = value.astype(bf16)
+    rest = value - high.astype(f32)
+    middle = rest.astype(bf16)
+    low = (rest - middle.astype(f32)).astype(bf16)
+    parts = [jnp.dot(part, order, preferred_element_type=f32) for part in (high, middle, low)]
+    return parts[0] + (parts[1] + parts[2])
+
+
+def pack_kernel(tiles, slabs, reads, owner, rowoff, coloff, images, field, light, order,
+                packed, count, slot, row, col, shard, probe, hold, used, insem, outsem):
     tile = lax.axis_index("tile")
     slab = lax.axis_index("slab")
     for k in range(reads):
@@ -80,7 +102,9 @@
     for s in range(2):
         for q in range(2):
             for h in range(3):
-                shard[2 * s + q, h] = field[s, q, :, h * LANES:(h + 1) * LANES]
+                shard[2 * s + q, h] = rearrange(field[s, q, :, lanes(h)], order[...])
+    for g in range(4):
+        probe[g] = rearrange(light[:, lanes(g)], order[...])
 
     def sender(i, found):
         base = (i * slabs + slab) * reads
@@ -101,7 +125,7 @@
         pltpu.make_async_copy(hold.at[k], packed.at[0, 0], outsem.at[k]).wait()
 
 
-def pack(owner, rowoff, coloff, images, field, tiles, slabs):
+def pack(owner, rowoff, coloff, images, field, light, tiles, slabs):
     reads, n, _ = images.shape
     rows = field.shape[2]
     return pl.pallas_call(
@@ -113,9 +137,10 @@
             jax.ShapeDtypeStruct((K + 1,), jnp.int32),
             jax.ShapeDtypeStruct((K + 1,), jnp.int32),
             jax.ShapeDtypeStruct((4, 3, rows, LANES), f32),
+            jax.ShapeDtypeStruct((4, n, LANES), f32),
         ),
-        in_specs=[smem, smem, smem, anyspace, vmem],
-        out_specs=(anyspace, smem, smem, smem, smem, vmem),
+        in_specs=[smem, smem, smem, anyspace, vmem, vmem, vmem],
+        out_specs=(anyspace, smem, smem, smem, smem, vmem, vmem),
         scratch_shapes=[
             pltpu.VMEM((reads, n, n), bf16),
             pltpu.SMEM((tiles,), jnp.int32),
@@ -123,7 +148,7 @@
             pltpu.SemaphoreType.DMA((reads,)),
         ],
         name="pack",
-    )(owner, rowoff, coloff, images, field)
+    )(owner, rowoff, coloff, images, field, light, lane_order())
 
 
 def product(ar, ai, br, bi):
@@ -138,51 +163,76 @@
     return slice(c * LANES, (c + 1) * LANES)
 
 
-def rows_of(p, b):
-    return slice(2 * HALF * p + HALF * b, 2 * HALF * p + HALF * b + HALF)
-
-
-def spread_rows(start, p, b):
-    return pl.ds(start + p + 2 * HALF * b, HALF, stride=2)
-
-
-def window(field, s, top, left, p, b, c):
-    where = spread_rows(top, p, b)
+def rows_of(p, b, r):
+    start = 2 * HALF * p + HALF * b + r
+    return slice(start, start + CHUNK)
+
+
+def spread_rows(start, p, b, r):
+    return pl.ds(start + p + 2 * HALF * b + 2 * r, CHUNK, stride=2)
+
+
+def window(field, s, top, left, p, b, r, c):
+    where = spread_rows(top, p, b, r)
     return field[2 * s, left + c, where, :], field[2 * s + 1, left + c, where, :]
 
 
-def put(x, p, b, c, parts):
-    x[rows_of(p, b), lanes(c)] = parts[0].astype(bf16)
-    x[rows_of(p, b), lanes(2 + c)] = parts[1].astype(bf16)
-
-
-def chirp(kernel, p, b, c):
-    return kernel[0, rows_of(p, b), lanes(c)], kernel[1, rows_of(p, b), lanes(c)]
-
-
-def lit(probe, p, b, c):
-    where = spread_rows(0, p, b)
+def put_natural(x, p, b, r, parts):
+    for c in range(2):
+        for q in range(2):
+            x[rows_of(p, b, r), lanes(2 * q + c)] = parts[c][q].astype(bf16)
+
+
+def put(x, p, b, r, parts):
+    low = lax.broadcasted_iota(jnp.int32, (CHUNK, LANES), 1) < HALF
+    for q in range(2):
+        near, far = parts[0][q], parts[1][q]
+        even = jnp.where(low, near, pltpu.roll(far, HALF, 1))
+        odd = jnp.where(low, pltpu.roll(near, HALF, 1), far)
+        x[0, rows_of(p, b, r), lanes(q)] = even.astype(bf16)
+        x[1, rows_of(p, b, r), lanes(q)] = odd.astype(bf16)
+
+
+def chirp(kernel, p, b, r, c):
+    return kernel[0, rows_of(p, b, r), lanes(c)], kernel[1, rows_of(p, b, r), lanes(c)]
+
+
+def lit(probe, p, b, r, c):
+    where = spread_rows(0, p, b, r)
     return probe[c, where, :], probe[2 + c, where, :]
 
 
 def each(y, use):
     for p in range(2):
-        for c in range(2):
-            parts = [y[HALF * k:HALF * k + HALF, lanes(c)] for k in (p, 2 + p, 4 + p, 6 + p)]
-            use(p, 0, c, parts[0] + parts[2], parts[1] + parts[3])
-            use(p, 1, c, parts[0] - parts[2], parts[1] - parts[3])
-
-
-def transform(x, h, y, right, left):
+        for r in range(0, HALF, CHUNK):
+            e = [[y[HALF * k + r:HALF * k + r + CHUNK, lanes(c)] for k in (p, 2 + p)] for c in range(2)]
+            o = [[y[HALF * k + r:HALF * k + r + CHUNK, lanes(c)] for k in (4 + p, 6 + p)] for c in range(2)]
+            use(p, 0, r, [(e[c][0] + o[c][0], e[c][1] + o[c][1]) for c in range(2)])
+            use(p, 1, r, [(e[c][0] - o[c][0], e[c][1] - o[c][1]) for c in range(2)])
+
+
+def finish_transform(h, y, low, high, left):
     n = 4 * HALF
     m = n // 2
-    half = jnp.dot(x[...], right[...], preferred_element_type=f32)
-    h[0:m, :] = half[:m, :n].astype(bf16)
-    h[m:n, :] = half[:m, n:].astype(bf16)
-    h[n:n + m, :] = half[m:, :n].astype(bf16)
-    h[n + m:, :] = half[m:, n:].astype(bf16)
+    for p in range(2):
+        for q in range(2):
+            where = slice(p * n + q * m, p * n + q * m + m)
+            h[where, lanes(0)] = low[p * m:p * m + m, lanes(q)].astype(bf16)
+            h[where, lanes(1)] = high[p * m:p * m + m, lanes(q)].astype(bf16)
     y[:n, :] = jnp.dot(left[0], h[:n, :], preferred_element_type=f32)
     y[n:, :] = jnp.dot(left[1], h[n:, :], preferred_element_type=f32)
+
+
+def transform(x, h, y, right, left):
+    even = jnp.dot(x[0], right[0], preferred_element_type=f32)
+    odd = jnp.dot(x[1], right[1], preferred_element_type=f32)
+    finish_transform(h, y, even + odd, even - odd, left)
+
+
+def transform_natural(x, h, y, right, left):
+    n = 4 * HALF
+    half = jnp.dot(x[...], right[...], preferred_element_type=f32)
+    finish_transform(h, y, half[:, :n], half[:, n:], left)
 
 
 def interleave(first, second, transforms):
@@ -196,13 +246,13 @@
 
 
 XORDER = (1, 3, 2)
-RELAY_STEPS = ((1, slice(3, 6)), (5, slice(6, 9)))
+RELAY_STEPS = ((1, slice(3, 5)), (2, slice(5, 6)), (3, slice(6, 7)), (4, slice(7, 8)), (5, slice(8, 9)))
 YORDER = (2, 1, 3)
 
 
-def exchange_kernel(tiles, slabs, cores, rows, packed, shard, slot, row, col, probe_in, rf, ri, lf, li, kernel,
+def exchange_kernel(tiles, slabs, cores, rows, packed, shard, slot, row, col, probe, right_forward, right_inverse, right_far, left_forward, left_inverse, kernel,
                     got, field_out, fars, waves,
-                    field, probe, x, h, y, far, wave, hold, localsem, outsem,
+                    field, x, h, y, far, wave, hold, localsem, outsem,
                     stage, xsend, xrecv, ysend, yrecv, nsend, nrecv, zsend, zrecv, csend, crecv):
     tile = lax.axis_index("tile")
     slab = lax.axis_index("slab")
@@ -297,8 +347,6 @@
     ]
     relays = list(zip(relays, onwards))
 
-    for g in range(4):
-        probe[g] = probe_in[:, lanes(g)]
     pass_on(0, own)
     relay(relays[:3])
     pass_on(1, following)
@@ -326,21 +374,24 @@
         def begin():
             for p in range(2):
                 for b in range(2):
-                    for c in range(2):
-                        put(xj, p, b, c, product(*lit(probe, p, b, c), *window(field, 0, top, left, p, b, c)))
-
-        def scatter(p, b, c, re, im):
-            put(xj, p, b, c, product(*chirp(kernel, p, b, c), re, im))
-
-        def enter(p, b, c, re, im):
-            wj[rows_of(p, b), lanes(c)] = re
-            wj[rows_of(p, b), lanes(2 + c)] = im
-            put(xj, p, b, c, product(re, im, *window(field, 1, top, left, p, b, c)))
+                    for r in range(0, HALF, CHUNK):
+                        put(xj, p, b, r, [
+                            product(*lit(probe, p, b, r, c), *window(field, 0, top, left, p, b, r, c)) for c in range(2)
+                        ])
+
+        def scatter(p, b, r, parts):
+            put(xj, p, b, r, [product(*chirp(kernel, p, b, r, c), *parts[c]) for c in range(2)])
+
+        def enter(p, b, r, parts):
+            for c in range(2):
+                wj[rows_of(p, b, r), lanes(c)] = parts[c][0]
+                wj[rows_of(p, b, r), lanes(2 + c)] = parts[c][1]
+            put(xj, p, b, r, [product(*parts[c], *window(field, 1, top, left, p, b, r, c)) for c in range(2)])
 
         return [
-            begin, lambda: transform(xj, hj, yj, rf, lf), lambda: each(yj, scatter),
-            lambda: transform(xj, hj, yj, ri, li), lambda: each(yj, enter),
-            lambda: transform(xj, hj, fj, rf, lf), lambda: None,
+            begin, lambda: transform(xj, hj, yj, right_forward, left_forward), lambda: each(yj, scatter),
+            lambda: transform(xj, hj, yj, right_inverse, left_inverse), lambda: each(yj, enter),
+            lambda: transform(xj, hj, fj, right_far, left_forward), lambda: None,
         ]
 
     def step(k, carry):
@@ -377,7 +428,7 @@
 
 
 def exchange(packed, shard, slot, row, col, probe, tables, tiles, slabs):
-    _, _, n, _ = packed.shape
+    n = packed.shape[2]
     planes, cols, rows, width = shard.shape
     cores = 2
     levels = slabs // cores
@@ -392,12 +443,11 @@
             jax.ShapeDtypeStruct((K, 2 * n, n), f32),
             jax.ShapeDtypeStruct((K, n, 2 * n), f32),
         ),
-        in_specs=[anyspace, vmem, smem, smem, smem] + [vmem] * 6,
+        in_specs=[anyspace, vmem, smem, smem, smem] + [vmem] * 7,
         out_specs=(anyspace,) * 4,
         scratch_shapes=[
             pltpu.VMEM(extended, f32),
-            pltpu.VMEM((4, n, width), f32),
-            pltpu.VMEM((2, n, 2 * n), bf16),
+            pltpu.VMEM((2, 2, n, n), bf16),
             pltpu.VMEM((2, 2 * n, n), bf16),
             pltpu.VMEM((2, 2 * n, n), f32),
             pltpu.VMEM((2, 2, 2 * n, n), f32),
@@ -414,16 +464,17 @@
         ],
         compiler_params=pltpu.CompilerParams(collective_id=0, has_side_effects=True, vmem_limit_bytes=VMEM_LIMIT),
         name="exchange",
-    )(packed, shard, slot, row, col, probe, *tables)
-
-
-def grad_kernel(count, slot, row, col, field, images, fars, waves, probe_in, rf, ri, lf, li, kernel,
-                total, x, h, y, far, wave, measured, probe, image, insem):
+    )(
+        packed, shard, slot, row, col, probe, tables["right_forward"], tables["right_inverse"], tables["right_far"],
+        tables["left_forward"], tables["left_inverse"], tables["kernel"],
+    )
+
+
+def grad_kernel(count, slot, row, col, field, images, fars, waves, probe, right_forward, right_inverse, right_back, left_forward, left_inverse, kernel,
+                out, total, x, xfull, h, y, far, wave, measured, image, insem, outsem):
     dump = field.shape[2]
     total[...] = jnp.zeros_like(total)
     live = count[0]
-    for g in range(4):
-        probe[g] = probe_in[:, lanes(g)]
 
     def inputs(i):
         index = slot[i]
@@ -439,37 +490,44 @@
         left = col[i]
         place = top if valid is None else jnp.where(valid, top, dump)
         at = lax.rem(i, 4)
+        xf = xfull.at[j]
         xj, hj, yj, mj = x.at[j], h.at[j], y.at[j], measured.at[j]
         wj, fj, source = wave.at[at], far.at[at], image.at[at]
 
-        def add(s, p, b, c, parts):
-            where = spread_rows(place, p, b)
-            total[2 * s, left + c, where, :] += parts[0]
-            total[2 * s + 1, left + c, where, :] += parts[1]
-
-        def compare(p, b, c, re, im):
-            misfit = re * re + im * im - mj[c, spread_rows(0, p, b), :]
-            put(xj, p, b, c, (re * misfit, im * misfit))
+        def add(s, p, b, r, parts):
+            where = spread_rows(place, p, b, r)
+            for c in range(2):
+                total[2 * s, left + c, where, :] += parts[c][0]
+                total[2 * s + 1, left + c, where, :] += parts[c][1]
+
+        def compare(p, b, r, parts):
+            scaled = []
+            for c in range(2):
+                re, im = parts[c]
+                misfit = re * re + im * im - mj[c, spread_rows(0, p, b, r), :]
+                scaled.append((re * misfit, im * misfit))
+            put_natural(xf, p, b, r, scaled)
 
         def compare_all():
             for c in range(2):
                 mj[c] = source[:, lanes(c)].astype(f32)
             each(fj, compare)
 
-        def leave(p, b, c, re, im):
-            add(1, p, b, c, conjugate_product(wj[rows_of(p, b), lanes(c)], wj[rows_of(p, b), lanes(2 + c)], re, im))
-            put(xj, p, b, c, conjugate_product(*window(field, 1, top, left, p, b, c), re, im))
-
-        def gather(p, b, c, re, im):
-            put(xj, p, b, c, conjugate_product(*chirp(kernel, p, b, c), re, im))
-
-        def finish(p, b, c, re, im):
-            add(0, p, b, c, conjugate_product(*lit(probe, p, b, c), re, im))
+        def leave(p, b, r, parts):
+            where = rows_of(p, b, r)
+            add(1, p, b, r, [conjugate_product(wj[where, lanes(c)], wj[where, lanes(2 + c)], *parts[c]) for c in range(2)])
+            put(xj, p, b, r, [conjugate_product(*window(field, 1, top, left, p, b, r, c), *parts[c]) for c in range(2)])
+
+        def gather(p, b, r, parts):
+            put(xj, p, b, r, [conjugate_product(*chirp(kernel, p, b, r, c), *parts[c]) for c in range(2)])
+
+        def finish(p, b, r, parts):
+            add(0, p, b, r, [conjugate_product(*lit(probe, p, b, r, c), *parts[c]) for c in range(2)])
 
         return [
-            compare_all, lambda: transform(xj, hj, yj, ri, li), lambda: each(yj, leave),
-            lambda: transform(xj, hj, yj, rf, lf), lambda: each(yj, gather),
-            lambda: transform(xj, hj, yj, ri, li), lambda: each(yj, finish),
+            compare_all, lambda: transform_natural(xf, hj, yj, right_back, left_inverse), lambda: each(yj, leave),
+            lambda: transform(xj, hj, yj, right_forward, left_forward), lambda: each(yj, gather),
+            lambda: transform(xj, hj, yj, right_inverse, left_inverse), lambda: each(yj, finish),
         ]
 
     def step(k, carry):
@@ -499,33 +557,41 @@
             for copy in inputs(s):
                 copy.start()
     lax.fori_loop(0, lax.div(live + 1, 2), step, 0)
+    store = pltpu.make_async_copy(total.at[:, :, :dump], out, outsem)
+    store.start()
+    store.wait()
 
 
 def gradient(count, slot, row, col, field, images, fars, waves, probe, tables):
-    n = probe.shape[0]
     planes, cols, rows, width = field.shape
+    n = probe.shape[1]
     return pl.pallas_call(
         grad_kernel,
-        out_shape=jax.ShapeDtypeStruct((planes, cols, rows + n, width), f32),
-        in_specs=[smem] * 4 + [vmem] + [anyspace] * 3 + [vmem] * 6,
-        out_specs=vmem,
+        out_shape=jax.ShapeDtypeStruct(field.shape, f32),
+        in_specs=[smem] * 4 + [vmem] + [anyspace] * 3 + [vmem] * 7,
+        out_specs=anyspace,
         scratch_shapes=[
+            pltpu.VMEM((planes, cols, rows + n, width), f32),
+            pltpu.VMEM((2, 2, n, n), bf16),
             pltpu.VMEM((2, n, 2 * n), bf16),
             pltpu.VMEM((2, 2 * n, n), bf16),
             pltpu.VMEM((2, 2 * n, n), f32),
             pltpu.VMEM((4, 2 * n, n), f32),
             pltpu.VMEM((4, n, 2 * n), f32),
             pltpu.VMEM((2, 2, n, width), f32),
-            pltpu.VMEM((4, n, width), f32),
             pltpu.VMEM((4, n, n), bf16),
             pltpu.SemaphoreType.DMA((4, 3)),
+            pltpu.SemaphoreType.DMA,
         ],
         compiler_params=pltpu.CompilerParams(vmem_limit_bytes=VMEM_LIMIT),
         name="gradient",
-    )(count, slot, row, col, field, images, fars, waves, probe, *tables)
-
-
-def reduce_kernel(tiles, slabs, cores, total, out, part, near, far, outgoing,
+    )(
+        count, slot, row, col, field, images, fars, waves, probe, tables["right_forward"], tables["right_inverse"],
+        tables["right_back"], tables["left_forward"], tables["left_inverse"], tables["kernel"],
+    )
+
+
+def reduce_kernel(tiles, slabs, cores, total, unsort, out, part, near, far, outgoing,
                   localsem, csend, crecv, zsend, zrecv, fsend, frecv):
     tile = lax.axis_index("tile")
     slab = lax.axis_index("slab")
@@ -596,21 +662,21 @@
             value = part[last, p, h] + near[last, p, h]
             for k in range(2 * levels - 1):
                 value = value + far[k, p, h].astype(f32)
-            out[p // 2, p % 2, :, h * LANES:(h + 1) * LANES] = value
+            out[p // 2, p % 2, :, lanes(h)] = rearrange(value, unsort[...])
 
 
 def reduce(total, tiles, slabs):
     cores = 2
     levels = slabs // cores
     planes, cols, rows, lanes = total.shape
-    each = (rows - 256) // (2 * slabs)
+    each = rows // (2 * slabs)
     sem = pltpu.SemaphoreType.DMA
     count = 2 * levels
     total = total.reshape(planes, cols, rows // (cores * each), cores, each, lanes)
     return pl.pallas_call(
         functools.partial(reduce_kernel, tiles, slabs, cores),
         out_shape=jax.ShapeDtypeStruct((2, 2, each, cols * lanes), f32),
-        in_specs=[anyspace],
+        in_specs=[anyspace, vmem],
         out_specs=vmem,
         scratch_shapes=[
             pltpu.VMEM((count, planes, cols, each, lanes), f32),
@@ -624,18 +690,18 @@
         ],
         compiler_params=pltpu.CompilerParams(collective_id=1, has_side_effects=True, vmem_limit_bytes=VMEM_LIMIT),
         name="reduce",
-    )(total)
+    )(total, lane_order().T)
 
 
 def shards(intensities, object_field, probe_wave, owner_tile, row_offset, col_offset):
     tiles = lax.axis_size("tile")
     slabs = lax.axis_size("slab")
-    packed, count, slot, row, col, shard = pack(
-        owner_tile, row_offset, col_offset, intensities, object_field, tiles, slabs
+    packed, count, slot, row, col, shard, probe = pack(
+        owner_tile, row_offset, col_offset, intensities, object_field, probe_wave, tiles, slabs
     )
     tables = make_tables(intensities.shape[1])
-    images, field, fars, waves = exchange(packed, shard, slot, row, col, probe_wave, tables, tiles, slabs)
-    total = gradient(count, slot, row, col, field, images, fars, waves, probe_wave, tables)
+    images, field, fars, waves = exchange(packed, shard, slot, row, col, probe, tables, tiles, slabs)
+    total = gradient(count, slot, row, col, field, images, fars, waves, probe, tables)
     return reduce(total, tiles, slabs)
 
 

time: 123 us -> 118 us (0.959)
  Pallas kernels: 121 us -> 116 us
    pallas_call x1, Pallas kernels: 65.8 us -> 59.1 us  [exchange(): pl.pallas_call(functools.partial(exchange_kernel, tiles, slabs, cores, ro...]
    pallas_call x1, Pallas kernels: 27.2 us -> 29.6 us  [gradient(): pl.pallas_call(grad_kernel, out_shape=jax.ShapeDtypeStruct(field.shape, f...]
    pallas_call x1, Pallas kernels: 23.1 us -> 21.7 us  [reduce(): pl.pallas_call(functools.partial(reduce_kernel, tiles, slabs, cores), out...]
where the time goes in v4:
time: 118 us
  Pallas kernels  116 us (98%)
  local copies, waits for them, and re-layouts  1.62 us (1%)
    pallas_call x1, Pallas kernels, exchange(): pl.pallas_call(functools.partial(exchange_kernel, tiles, slabs, cores, ro...  59.1 us
    pallas_call x1, Pallas kernels, gradient(): pl.pallas_call(grad_kernel, out_shape=jax.ShapeDtypeStruct(field.shape, f...  29.6 us
    pallas_call x1, Pallas kernels, reduce(): pl.pallas_call(functools.partial(reduce_kernel, tiles, slabs, cores), out...  21.7 us
    pallas_call x1, Pallas kernels, pack(): pl.pallas_call(functools.partial(pack_kernel, tiles, slabs, reads), out_s...  5.65 us

profile of v4, /device:TPU:1, one launch (start us, length us, event | category | flops | bytes accessed | tf_op | source)
XLA Modules:
  0.0 117.6 jit_solution(13741519799120883307)
XLA Ops:
  0.0 5.6 %pack.1 = (bf16[16,2,256,256]{3,2,1,0:T(8,128)(2,1)}, s32[1]{0:T(128)}, s32[17]{0:T(128)}, s32[17]{0:T(128)}, s32[17]{0:T(128)}, /*index=5*/f32[4,3,32,128]{3,2,1,0:T(8,128)}, f32[4,256,128]{2,1,0:T(8,128)}) custom-call(s32[1792]{0:T(1024)} %owner.1, s32[1792]{0:T(1024)} %rowoff.1, s32[1792]{0:T(1024)} %coloff.1, bf16[14,256,256]{2,1,0:T(8,128)(2,1)} %images.1, ...), custom_call_target="tpu_custom_call" | custom-call | tf_op jit(solution)/shard_map/pack/pallas_call | solution.py:131
  5.7 59.1 %exchange.1 = (bf16[16,2,256,256]{3,2,1,0:T(8,128)(2,1)}, f32[4,3,512,128]{3,2,1,0:T(8,128)}, f32[16,512,256]{2,1,0:T(8,128)}, f32[16,256,512]{2,1,0:T(8,128)}) custom-call(bf16[16,2,256,256]{3,2,1,0:T(8,128)(2,1)} %get-tuple-element.20.packed, f32[4,3,32,128]{3,2,1,0:T(8,128)} %get-tuple-element.21.shard, s32[17]{0:T(128)} %get-tuple-element.17.slot, ...), custom_call_target="tpu_custom_call" | custom-call | tf_op jit(solution)/shard_map/exchange/pallas_call | solution.py:438
  64.7 29.6 %gradient.1 = f32[4,3,512,128]{3,2,1,0:T(8,128)} custom-call(s32[1]{0:T(128)} %get-tuple-element.16.count, s32[17]{0:T(128)} %get-tuple-element.17.slot, s32[17]{0:T(128)} %get-tuple-element.18.row, s32[17]{0:T(128)} %get-tuple-element.19.col, f32[4,3,512,128]{3,2,1,0:T(8,128)} %get-tuple-element.23.field, ...), custom_call_target="tpu_custom_call" | custom-call | tf_op jit(solution)/shard_map/gradient/pallas_call | solution.py:568
  94.3 21.7 %reduce.1 = f32[2,2,32,384]{3,2,1,0:T(8,128)} custom-call(f32[4,3,8,2,32,128]{5,4,3,2,1,0:T(8,128)} %bitcast.1, bf16[128,128]{1,0:T(8,128)(2,1)} %constant.26.unsort), custom_call_target="tpu_custom_call" | custom-call | tf_op jit(solution)/shard_map/reduce/pallas_call | solution.py:676
  116.0 1.6 %copy.17 = f32[2,2,32,384]{3,2,1,0:T(8,128)} copy(f32[2,2,32,384]{3,2,1,0:T(8,128)} %reduce.1) | data formatting | bytes 393216

commit v5 on v4

--- a/solution.py
+++ b/solution.py
@@ -470,8 +470,23 @@
     )
 
 
+def together(*groups):
+    steps = max(len(group) for group in groups)
+    for i in range(steps):
+        for group in groups:
+            for unit in group[i * len(group) // steps:(i + 1) * len(group) // steps]:
+                unit()
+
+
+def each_part(y, use, p, r):
+    e = [[y[HALF * k + r:HALF * k + r + CHUNK, lanes(c)] for k in (p, 2 + p)] for c in range(2)]
+    o = [[y[HALF * k + r:HALF * k + r + CHUNK, lanes(c)] for k in (4 + p, 6 + p)] for c in range(2)]
+    use(p, 0, r, [(e[c][0] + o[c][0], e[c][1] + o[c][1]) for c in range(2)])
+    use(p, 1, r, [(e[c][0] - o[c][0], e[c][1] - o[c][1]) for c in range(2)])
+
+
 def grad_kernel(count, slot, row, col, field, images, fars, waves, probe, right_forward, right_inverse, right_back, left_forward, left_inverse, kernel,
-                out, total, x, xfull, h, y, far, wave, measured, image, insem, outsem):
+                out, total, x, xfull, h, far, wave, measured, image, insem, outsem):
     dump = field.shape[2]
     total[...] = jnp.zeros_like(total)
     live = count[0]
@@ -485,13 +500,12 @@
             pltpu.make_async_copy(waves.at[i], wave.at[place], insem.at[place, 2]),
         )
 
-    def pattern(i, j, valid):
+    def pattern(i, j, valid, accs):
         top = row[i]
         left = col[i]
         place = top if valid is None else jnp.where(valid, top, dump)
         at = lax.rem(i, 4)
-        xf = xfull.at[j]
-        xj, hj, yj, mj = x.at[j], h.at[j], y.at[j], measured.at[j]
+        xj, xf, hj, mj = x.at[j], xfull.at[j], h.at[j], measured.at[j]
         wj, fj, source = wave.at[at], far.at[at], image.at[at]
 
         def add(s, p, b, r, parts):
@@ -508,11 +522,6 @@
                 scaled.append((re * misfit, im * misfit))
             put_natural(xf, p, b, r, scaled)
 
-        def compare_all():
-            for c in range(2):
-                mj[c] = source[:, lanes(c)].astype(f32)
-            each(fj, compare)
-
         def leave(p, b, r, parts):
             where = rows_of(p, b, r)
             add(1, p, b, r, [conjugate_product(wj[where, lanes(c)], wj[where, lanes(2 + c)], *parts[c]) for c in range(2)])
@@ -524,10 +533,86 @@
         def finish(p, b, r, parts):
             add(0, p, b, r, [conjugate_product(*lit(probe, p, b, r, c), *parts[c]) for c in range(2)])
 
-        return [
-            compare_all, lambda: transform_natural(xf, hj, yj, right_back, left_inverse), lambda: each(yj, leave),
-            lambda: transform(xj, hj, yj, right_forward, left_forward), lambda: each(yj, gather),
-            lambda: transform(xj, hj, yj, right_inverse, left_inverse), lambda: each(yj, finish),
+        n = 4 * HALF
+        units = n // CHUNK
+        acc = [accs[(2 * j + u) * units:(2 * j + u + 1) * units] for u in range(2)]
+
+        def compare_units():
+            def convert():
+                for c in range(2):
+                    mj[c] = source[:, lanes(c)].astype(f32)
+
+            return [convert] + [functools.partial(each_part, fj, compare, p, r) for p in range(2) for r in range(0, HALF, CHUNK)]
+
+        def push(first, second):
+            pltpu.matmul_push_rhs(first, j, 0)
+            pltpu.matmul_push_rhs(second, j, 1)
+
+        def feed(i, first, second, load):
+            pltpu.matmul_acc_lhs(acc[0][i], first, j if load else None)
+            pltpu.matmul_acc_lhs(acc[1][i], second, j if load else None)
+
+        def rows(i):
+            return slice(i * CHUNK, (i + 1) * CHUNK)
+
+        def right_units(right):
+            def unit(i):
+                if i == 0:
+                    push(right[0], right[1])
+                feed(i, xj[0, rows(i), :], xj[1, rows(i), :], i == 0)
+
+            return [functools.partial(unit, i) for i in range(units)]
+
+        def back_units():
+            def unit(t, i):
+                if i == 0:
+                    push(right_back[t * n:(t + 1) * n, :n], right_back[t * n:(t + 1) * n, n:])
+                part = xf[rows(i), t * n:(t + 1) * n]
+                feed(i, part, part, i == 0)
+
+            return [functools.partial(unit, t, i) for t in range(2) for i in range(units)]
+
+        def half_units(split):
+            def unit(i):
+                low = pltpu.matmul_pop(acc[0][i])
+                high = pltpu.matmul_pop(acc[1][i])
+                if split:
+                    low, high = low + high, low - high
+                m = n // 2
+                p, start = divmod(i * CHUNK, m)
+                for q in range(2):
+                    where = slice(p * n + q * m + start, p * n + q * m + start + CHUNK)
+                    hj[where, lanes(0)] = low[:, lanes(q)].astype(bf16)
+                    hj[where, lanes(1)] = high[:, lanes(q)].astype(bf16)
+
+            return [functools.partial(unit, i) for i in range(units)]
+
+        order = [(p, r) for p in range(2) for r in range(0, HALF, CHUNK)]
+
+        def left_units(left):
+            def unit(i):
+                if i == 0:
+                    push(hj[:n, :], hj[n:, :])
+                p, r = order[i // 2]
+                start = (i % 2) * 2 * HALF + p * HALF + r
+                feed(i, left[0, start:start + CHUNK, :], left[1, start:start + CHUNK, :], i == 0)
+
+            return [functools.partial(unit, i) for i in range(units)]
+
+        def use_units(use):
+            def unit(i):
+                p, r = order[i]
+                e = [pltpu.matmul_pop(acc[0][2 * i + q]) for q in range(2)]
+                o = [pltpu.matmul_pop(acc[1][2 * i + q]) for q in range(2)]
+                use(p, 0, r, [(e[0][:, lanes(c)] + o[0][:, lanes(c)], e[1][:, lanes(c)] + o[1][:, lanes(c)]) for c in range(2)])
+                use(p, 1, r, [(e[0][:, lanes(c)] - o[0][:, lanes(c)], e[1][:, lanes(c)] - o[1][:, lanes(c)]) for c in range(2)])
+
+            return [functools.partial(unit, i) for i in range(len(order))]
+
+        return compare_units(), [
+            (back_units(), half_units(False)), (left_units(left_inverse), use_units(leave)),
+            (right_units(right_forward), half_units(True)), (left_units(left_forward), use_units(gather)),
+            (right_units(right_inverse), half_units(True)), (left_units(left_inverse), use_units(finish)),
         ]
 
     def step(k, carry):
@@ -548,7 +633,19 @@
                 for copy in inputs(2 * k + ahead):
                     copy.start()
 
-        interleave(pattern(a, 0, None), pattern(b, 1, valid), 3)
+        def both(*accs):
+            first_compare, first = pattern(a, 0, None, accs)
+            second_compare, second = pattern(b, 1, valid, accs)
+            together(first_compare)
+            together(first[0][0], second_compare)
+            for s in range(len(first)):
+                together(second[s][0], first[s][1])
+                together(first[s + 1][0] if s + 1 < len(first) else [], second[s][1])
+
+        n = 4 * HALF
+        pl.run_scoped(both, *[
+            pltpu.ACC(mxu_id=u)((CHUNK, n), f32) for _ in range(2) for u in range(2) for _ in range(n // CHUNK)
+        ])
         return carry
 
     for s in range(2):
@@ -575,7 +672,6 @@
             pltpu.VMEM((2, 2, n, n), bf16),
             pltpu.VMEM((2, n, 2 * n), bf16),
             pltpu.VMEM((2, 2 * n, n), bf16),
-            pltpu.VMEM((2, 2 * n, n), f32),
             pltpu.VMEM((4, 2 * n, n), f32),
             pltpu.VMEM((4, n, 2 * n), f32),
             pltpu.VMEM((2, 2, n, width), f32),

time: 118 us -> 114 us (0.966)
  Pallas kernels: 116 us -> 111 us
    pallas_call x1, Pallas kernels: 29.6 us -> 23.1 us  [gradient(): pl.pallas_call(grad_kernel, out_shape=jax.ShapeDtypeStruct(field.shape, f...]
    pallas_call x1, Pallas kernels: 21.7 us -> 23.6 us  [reduce(): pl.pallas_call(functools.partial(reduce_kernel, tiles, slabs, cores), out...]
where the time goes in v5:
time: 114 us; the launch traced here: 113 us
  Pallas kernels  111 us (97%)
  local copies, waits for them, and re-layouts  1.62 us (1%)
    pallas_call x1, Pallas kernels, exchange(): pl.pallas_call(functools.partial(exchange_kernel, tiles, slabs, cores, ro...  59.1 us
    pallas_call x1, Pallas kernels, reduce(): pl.pallas_call(functools.partial(reduce_kernel, tiles, slabs, cores), out...  23.6 us
    pallas_call x1, Pallas kernels, gradient(): pl.pallas_call(grad_kernel, out_shape=jax.ShapeDtypeStruct(field.shape, f...  23.1 us
    pallas_call x1, Pallas kernels, pack(): pl.pallas_call(functools.partial(pack_kernel, tiles, slabs, reads), out_s...  5.65 us

profile of v5, /device:TPU:1, one launch (start us, length us, event | category | flops | bytes accessed | tf_op | source)
XLA Modules:
  0.0 113.0 jit_solution(8310701803376900845)
XLA Ops:
  0.0 5.6 %pack.1 = (bf16[16,2,256,256]{3,2,1,0:T(8,128)(2,1)}, s32[1]{0:T(128)}, s32[17]{0:T(128)}, s32[17]{0:T(128)}, s32[17]{0:T(128)}, /*index=5*/f32[4,3,32,128]{3,2,1,0:T(8,128)}, f32[4,256,128]{2,1,0:T(8,128)}) custom-call(s32[1792]{0:T(1024)} %owner.1, s32[1792]{0:T(1024)} %rowoff.1, s32[1792]{0:T(1024)} %coloff.1, bf16[14,256,256]{2,1,0:T(8,128)(2,1)} %images.1, ...), custom_call_target="tpu_custom_call" | custom-call | tf_op jit(solution)/shard_map/pack/pallas_call | solution.py:131
  5.7 59.1 %exchange.1 = (bf16[16,2,256,256]{3,2,1,0:T(8,128)(2,1)}, f32[4,3,512,128]{3,2,1,0:T(8,128)}, f32[16,512,256]{2,1,0:T(8,128)}, f32[16,256,512]{2,1,0:T(8,128)}) custom-call(bf16[16,2,256,256]{3,2,1,0:T(8,128)(2,1)} %get-tuple-element.20.packed, f32[4,3,32,128]{3,2,1,0:T(8,128)} %get-tuple-element.21.shard, s32[17]{0:T(128)} %get-tuple-element.17.slot, ...), custom_call_target="tpu_custom_call" | custom-call | tf_op jit(solution)/shard_map/exchange/pallas_call | solution.py:438
  64.7 23.1 %gradient.1 = f32[4,3,512,128]{3,2,1,0:T(8,128)} custom-call(s32[1]{0:T(128)} %get-tuple-element.16.count, s32[17]{0:T(128)} %get-tuple-element.17.slot, s32[17]{0:T(128)} %get-tuple-element.18.row, s32[17]{0:T(128)} %get-tuple-element.19.col, f32[4,3,512,128]{3,2,1,0:T(8,128)} %get-tuple-element.23.field, ...), custom_call_target="tpu_custom_call" | custom-call | tf_op jit(solution)/shard_map/gradient/pallas_call | solution.py:665
  87.8 23.6 %reduce.1 = f32[2,2,32,384]{3,2,1,0:T(8,128)} custom-call(f32[4,3,8,2,32,128]{5,4,3,2,1,0:T(8,128)} %bitcast.1, bf16[128,128]{1,0:T(8,128)(2,1)} %constant.26.unsort), custom_call_target="tpu_custom_call" | custom-call | tf_op jit(solution)/shard_map/reduce/pallas_call | solution.py:772
  111.4 1.6 %copy.17 = f32[2,2,32,384]{3,2,1,0:T(8,128)} copy(f32[2,2,32,384]{3,2,1,0:T(8,128)} %reduce.1) | data formatting | bytes 393216

commit v6 on v5

--- a/solution.py
+++ b/solution.py
@@ -81,14 +81,13 @@
     return parts[0] + (parts[1] + parts[2])
 
 
-def pack_kernel(tiles, slabs, reads, owner, rowoff, coloff, images, field, light, order,
-                packed, count, slot, row, col, shard, probe, hold, used, insem, outsem):
+def route_kernel(tiles, slabs, reads, owner, rowoff, coloff, pick, count, slot, row, col, used):
     tile = lax.axis_index("tile")
     slab = lax.axis_index("slab")
-    for k in range(reads):
-        pltpu.make_async_copy(images.at[k], hold.at[k], insem.at[k]).start()
     for t in range(tiles):
         used[t] = 0
+    for k in range(tiles * CAP):
+        pick[k] = 0
     for k in range(K + 1):
         slot[k] = 0
         row[k] = 0
@@ -97,14 +96,7 @@
         dest = owner[(tile * slabs + slab) * reads + k]
         rank = used[dest]
         used[dest] = rank + 1
-        pltpu.make_async_copy(images.at[k], hold.at[k], insem.at[k]).wait()
-        pltpu.make_async_copy(hold.at[k], packed.at[dest, rank], outsem.at[k]).start()
-    for s in range(2):
-        for q in range(2):
-            for h in range(3):
-                shard[2 * s + q, h] = rearrange(field[s, q, :, lanes(h)], order[...])
-    for g in range(4):
-        probe[g] = rearrange(light[:, lanes(g)], order[...])
+        pick[dest * CAP + rank] = k
 
     def sender(i, found):
         base = (i * slabs + slab) * reads
@@ -121,34 +113,18 @@
         return lax.fori_loop(0, reads, one, (found, jnp.int32(0)), unroll=True)[0]
 
     count[0] = lax.fori_loop(0, tiles, sender, jnp.int32(0))
-    for k in range(reads):
-        pltpu.make_async_copy(hold.at[k], packed.at[0, 0], outsem.at[k]).wait()
-
-
-def pack(owner, rowoff, coloff, images, field, light, tiles, slabs):
-    reads, n, _ = images.shape
-    rows = field.shape[2]
+
+
+def route(owner, rowoff, coloff, reads, tiles, slabs):
+    sizes = (tiles * CAP, 1, K + 1, K + 1, K + 1)
     return pl.pallas_call(
-        functools.partial(pack_kernel, tiles, slabs, reads),
-        out_shape=(
-            jax.ShapeDtypeStruct((tiles, CAP, n, n), bf16),
-            jax.ShapeDtypeStruct((1,), jnp.int32),
-            jax.ShapeDtypeStruct((K + 1,), jnp.int32),
-            jax.ShapeDtypeStruct((K + 1,), jnp.int32),
-            jax.ShapeDtypeStruct((K + 1,), jnp.int32),
-            jax.ShapeDtypeStruct((4, 3, rows, LANES), f32),
-            jax.ShapeDtypeStruct((4, n, LANES), f32),
-        ),
-        in_specs=[smem, smem, smem, anyspace, vmem, vmem, vmem],
-        out_specs=(anyspace, smem, smem, smem, smem, vmem, vmem),
-        scratch_shapes=[
-            pltpu.VMEM((reads, n, n), bf16),
-            pltpu.SMEM((tiles,), jnp.int32),
-            pltpu.SemaphoreType.DMA((reads,)),
-            pltpu.SemaphoreType.DMA((reads,)),
-        ],
-        name="pack",
-    )(owner, rowoff, coloff, images, field, light, lane_order())
+        functools.partial(route_kernel, tiles, slabs, reads),
+        out_shape=tuple(jax.ShapeDtypeStruct((size,), jnp.int32) for size in sizes),
+        in_specs=[smem, smem, smem],
+        out_specs=(smem,) * 5,
+        scratch_shapes=[pltpu.SMEM((tiles,), jnp.int32)],
+        name="route",
+    )(owner, rowoff, coloff)
 
 
 def product(ar, ai, br, bi):
@@ -250,9 +226,10 @@
 YORDER = (2, 1, 3)
 
 
-def exchange_kernel(tiles, slabs, cores, rows, packed, shard, slot, row, col, probe, right_forward, right_inverse, right_far, left_forward, left_inverse, kernel,
-                    got, field_out, fars, waves,
-                    field, x, h, y, far, wave, hold, localsem, outsem,
+def exchange_kernel(tiles, slabs, cores, rows, images, block_in, light, sort, pick, row, col,
+                    right_forward, right_inverse, right_far, left_forward, left_inverse, kernel,
+                    got, field_out, fars, waves, probe,
+                    field, x, h, y, far, wave, pictures, packed, shard, localsem, outsem, insem,
                     stage, xsend, xrecv, ysend, yrecv, nsend, nrecv, zsend, zrecv, csend, crecv):
     tile = lax.axis_index("tile")
     slab = lax.axis_index("slab")
@@ -272,6 +249,23 @@
     for d in range(1, levels):
         greet(tile, lax.rem(level + d, levels) * cores + core)
     greet(tile, other)
+    reads = images.shape[0]
+    loads = [pltpu.make_async_copy(images.at[k], pictures.at[k], insem.at[k]) for k in range(reads)]
+    for load in loads:
+        load.start()
+    for s in range(2):
+        for q in range(2):
+            for c in range(3):
+                shard[2 * s + q, c] = rearrange(block_in[s, q, :, lanes(c)], sort[...])
+    for load in loads:
+        load.wait()
+
+    def fill(t, carry):
+        for k in range(CAP):
+            packed[t, k] = pictures[pick[t * CAP + k]]
+        return carry
+
+    lax.fori_loop(0, tiles, fill, 0)
     pl.semaphore_wait(barrier, tiles + levels - 1)
 
     height = rows * slabs
@@ -329,11 +323,10 @@
         push(packed.at[at(0, dx)], got.at[tile], xsend.at[0, dx - 1], xrecv.at[0, dx - 1], at(0, dx), slab)
     keep = pltpu.make_async_copy(shard, block(0, slab), localsem.at[0])
     keep.start()
-    first = pltpu.make_async_copy(packed.at[tile], hold, localsem.at[1])
-    first.start()
-    first.wait()
-    second = pltpu.make_async_copy(hold, got.at[tile], localsem.at[1])
+    second = pltpu.make_async_copy(packed.at[tile], got.at[tile], localsem.at[1])
     second.start()
+    for g in range(4):
+        probe[g] = rearrange(light[:, lanes(g)], sort[...])
     ahead.wait_recv()
     following = share(1, block(1, slab), 1)
     def relay(part):
@@ -427,9 +420,10 @@
             copy.wait_recv()
 
 
-def exchange(packed, shard, slot, row, col, probe, tables, tiles, slabs):
-    n = packed.shape[2]
-    planes, cols, rows, width = shard.shape
+def exchange(images, block, light, pick, row, col, tables, tiles, slabs):
+    reads, n, _ = images.shape
+    rows = block.shape[2]
+    planes, cols, width = 4, block.shape[3] // LANES, LANES
     cores = 2
     levels = slabs // cores
     side = math.isqrt(tiles)
@@ -438,13 +432,14 @@
     return pl.pallas_call(
         functools.partial(exchange_kernel, tiles, slabs, cores, rows),
         out_shape=(
-            jax.ShapeDtypeStruct(packed.shape, packed.dtype),
+            jax.ShapeDtypeStruct((tiles, CAP, n, n), bf16),
             jax.ShapeDtypeStruct(extended, f32),
             jax.ShapeDtypeStruct((K, 2 * n, n), f32),
             jax.ShapeDtypeStruct((K, n, 2 * n), f32),
+            jax.ShapeDtypeStruct((4, n, width), f32),
         ),
-        in_specs=[anyspace, vmem, smem, smem, smem] + [vmem] * 7,
-        out_specs=(anyspace,) * 4,
+        in_specs=[anyspace, vmem, vmem, vmem, smem, smem, smem] + [vmem] * 6,
+        out_specs=(anyspace,) * 4 + (vmem,),
         scratch_shapes=[
             pltpu.VMEM(extended, f32),
             pltpu.VMEM((2, 2, n, n), bf16),
@@ -452,9 +447,12 @@
             pltpu.VMEM((2, 2 * n, n), f32),
             pltpu.VMEM((2, 2, 2 * n, n), f32),
             pltpu.VMEM((2, 2, n, 2 * n), f32),
-            pltpu.VMEM((CAP, n, n), bf16),
+            pltpu.VMEM((reads, n, n), bf16),
+            pltpu.VMEM((tiles, CAP, n, n), bf16),
+            pltpu.VMEM((planes, cols, rows, width), f32),
             sem((2,)),
             sem((2, 2, 2)),
+            sem((reads,)),
             pltpu.VMEM((side - 1, side - 1, CAP, n, n), bf16),
             sem((side, side - 1)), sem((side, side - 1)),
             sem((side, side - 1)), sem((side, side - 1)),
@@ -465,7 +463,8 @@
         compiler_params=pltpu.CompilerParams(collective_id=0, has_side_effects=True, vmem_limit_bytes=VMEM_LIMIT),
         name="exchange",
     )(
-        packed, shard, slot, row, col, probe, tables["right_forward"], tables["right_inverse"], tables["right_far"],
+        images, block, light, lane_order(), pick, row, col,
+        tables["right_forward"], tables["right_inverse"], tables["right_far"],
         tables["left_forward"], tables["left_inverse"], tables["kernel"],
     )
 
@@ -792,11 +791,13 @@
 def shards(intensities, object_field, probe_wave, owner_tile, row_offset, col_offset):
     tiles = lax.axis_size("tile")
     slabs = lax.axis_size("slab")
-    packed, count, slot, row, col, shard, probe = pack(
-        owner_tile, row_offset, col_offset, intensities, object_field, probe_wave, tiles, slabs
+    pick, count, slot, row, col = route(
+        owner_tile, row_offset, col_offset, intensities.shape[0], tiles, slabs
     )
     tables = make_tables(intensities.shape[1])
-    images, field, fars, waves = exchange(packed, shard, slot, row, col, probe, tables, tiles, slabs)
+    images, field, fars, waves, probe = exchange(
+        intensities, object_field, probe_wave, pick, row, col, tables, tiles, slabs
+    )
     total = gradient(count, slot, row, col, field, images, fars, waves, probe, tables)
     return reduce(total, tiles, slabs)
 

time: 114 us -> 112 us (0.982)
    pallas_call x1, Pallas kernels: 5.65 us -> 2.87 us  [route(): pl.pallas_call(functools.partial(route_kernel, tiles, slabs, reads), out_...]
where the time goes in v6:
time: 112 us
  Pallas kernels  110 us (98%)
  local copies, waits for them, and re-layouts  1.62 us (1%)
    pallas_call x1, Pallas kernels, exchange(): pl.pallas_call(functools.partial(exchange_kernel, tiles, slabs, cores, ro...  60 us
    pallas_call x1, Pallas kernels, reduce(): pl.pallas_call(functools.partial(reduce_kernel, tiles, slabs, cores), out...  24 us
    pallas_call x1, Pallas kernels, gradient(): pl.pallas_call(grad_kernel, out_shape=jax.ShapeDtypeStruct(field.shape, f...  23.1 us
    pallas_call x1, Pallas kernels, route(): pl.pallas_call(functools.partial(route_kernel, tiles, slabs, reads), out_...  2.87 us

profile of v6, /device:TPU:1, one launch (start us, length us, event | category | flops | bytes accessed | tf_op | source)
XLA Modules:
  0.0 111.6 jit_solution(13763316221540284624)
XLA Ops:
  0.0 2.9 %route.1 = (s32[32]{0:T(128)}, s32[1]{0:T(128)}, s32[17]{0:T(128)}, s32[17]{0:T(128)}, s32[17]{0:T(128)}) custom-call(s32[1792]{0:T(1024)} %owner.1, s32[1792]{0:T(1024)} %rowoff.1, s32[1792]{0:T(1024)} %coloff.1), custom_call_target="tpu_custom_call" | custom-call | tf_op jit(solution)/shard_map/route/pallas_call | solution.py:120
  2.9 60.0 %exchange.1 = (bf16[16,2,256,256]{3,2,1,0:T(8,128)(2,1)}, f32[4,3,512,128]{3,2,1,0:T(8,128)}, f32[16,512,256]{2,1,0:T(8,128)}, f32[16,256,512]{2,1,0:T(8,128)}, f32[4,256,128]{2,1,0:T(8,128)}) custom-call(bf16[14,256,256]{2,1,0:T(8,128)(2,1)} %images.1, f32[2,2,32,384]{3,2,1,0:T(8,128)} %block_in.1, f32[256,512]{1,0:T(8,128)} %light.1, ...), custom_call_target="tpu_custom_call" | custom-call | tf_op jit(solution)/shard_map/exchange/pallas_call | solution.py:432
  62.9 23.1 %gradient.1 = f32[4,3,512,128]{3,2,1,0:T(8,128)} custom-call(s32[1]{0:T(128)} %get-tuple-element.15.count, s32[17]{0:T(128)} %get-tuple-element.16.slot, s32[17]{0:T(128)} %get-tuple-element.17.row, s32[17]{0:T(128)} %get-tuple-element.18.col, f32[4,3,512,128]{3,2,1,0:T(8,128)} %get-tuple-element.20.field, ...), custom_call_target="tpu_custom_call" | custom-call | tf_op jit(solution)/shard_map/gradient/pallas_call | solution.py:664
  86.0 24.0 %reduce.1 = f32[2,2,32,384]{3,2,1,0:T(8,128)} custom-call(f32[4,3,8,2,32,128]{5,4,3,2,1,0:T(8,128)} %bitcast.1, bf16[128,128]{1,0:T(8,128)(2,1)} %constant.26.unsort), custom_call_target="tpu_custom_call" | custom-call | tf_op jit(solution)/shard_map/reduce/pallas_call | solution.py:771
  110.0 1.6 %copy.17 = f32[2,2,32,384]{3,2,1,0:T(8,128)} copy(f32[2,2,32,384]{3,2,1,0:T(8,128)} %reduce.1) | data formatting | bytes 393216

commit v7 on v6

--- a/solution.py
+++ b/solution.py
@@ -18,7 +18,7 @@
 CHIRP = 40.0
 LANES = 128
 HALF = 64
-CHUNK = 32
+CHUNK = 16
 VMEM_LIMIT = 60 * 2**20
 
 smem = pl.BlockSpec(memory_space=pltpu.SMEM)
@@ -472,7 +472,7 @@
 def together(*groups):
     steps = max(len(group) for group in groups)
     for i in range(steps):
-        for group in groups:
+        for group in groups[::-1]:
             for unit in group[i * len(group) // steps:(i + 1) * len(group) // steps]:
                 unit()
 
@@ -708,14 +708,18 @@
         place = lax.rem(level + d, levels) * cores + core
         greet(following, place)
         greet(preceding, place)
-    pl.semaphore_wait(barrier, 1 + levels - 1 + 2 * levels)
-
     def block(which, d):
         return which * levels + lax.rem(level + d, levels)
 
     order = [(1, 2), (1, 1), (1, 3), (0, 2), (0, 1), (0, 3), (1, 0), (0, 0)]
+    takes = []
+    for k, (which, d) in enumerate(order):
+        take = pltpu.make_async_copy(total.at[:, :, block(which, d), core], part.at[k], localsem.at[k])
+        take.start()
+        takes.append(take)
+    pl.semaphore_wait(barrier, 1 + levels - 1 + 2 * levels)
+
     swaps = []
-    takes = []
     for k, (which, d) in enumerate(order):
         b = block(which, d)
         copy = pltpu.make_async_remote_copy(
@@ -724,9 +728,6 @@
         )
         copy.start()
         swaps.append(copy)
-        take = pltpu.make_async_copy(total.at[:, :, b, core], part.at[k], localsem.at[k])
-        take.start()
-        takes.append(take)
     sends = []
     for k, (which, d) in enumerate(order):
         takes[k].wait()

time: 112 us -> 109 us (0.973)
  Pallas kernels: 110 us -> 107 us
    pallas_call x1, Pallas kernels: 24 us -> 22.5 us  [reduce(): pl.pallas_call(functools.partial(reduce_kernel, tiles, slabs, cores), out...]
    pallas_call x1, Pallas kernels: 23.1 us -> 21.9 us  [gradient(): pl.pallas_call(grad_kernel, out_shape=jax.ShapeDtypeStruct(field.shape, f...]
where the time goes in v7:
time: 109 us
  Pallas kernels  107 us (98%)
  local copies, waits for them, and re-layouts  1.62 us (1%)
    pallas_call x1, Pallas kernels, exchange(): pl.pallas_call(functools.partial(exchange_kernel, tiles, slabs, cores, ro...  60 us
    pallas_call x1, Pallas kernels, reduce(): pl.pallas_call(functools.partial(reduce_kernel, tiles, slabs, cores), out...  22.5 us
    pallas_call x1, Pallas kernels, gradient(): pl.pallas_call(grad_kernel, out_shape=jax.ShapeDtypeStruct(field.shape, f...  21.9 us
    pallas_call x1, Pallas kernels, route(): pl.pallas_call(functools.partial(route_kernel, tiles, slabs, reads), out_...  2.87 us

profile of v7, /device:TPU:1, one launch (start us, length us, event | category | flops | bytes accessed | tf_op | source)
XLA Modules:
  0.0 108.9 jit_solution(9731419069501105911)
XLA Ops:
  0.0 2.9 %route.1 = (s32[32]{0:T(128)}, s32[1]{0:T(128)}, s32[17]{0:T(128)}, s32[17]{0:T(128)}, s32[17]{0:T(128)}) custom-call(s32[1792]{0:T(1024)} %owner.1, s32[1792]{0:T(1024)} %rowoff.1, s32[1792]{0:T(1024)} %coloff.1), custom_call_target="tpu_custom_call" | custom-call | tf_op jit(solution)/shard_map/route/pallas_call | solution.py:120
  2.9 60.0 %exchange.1 = (bf16[16,2,256,256]{3,2,1,0:T(8,128)(2,1)}, f32[4,3,512,128]{3,2,1,0:T(8,128)}, f32[16,512,256]{2,1,0:T(8,128)}, f32[16,256,512]{2,1,0:T(8,128)}, f32[4,256,128]{2,1,0:T(8,128)}) custom-call(bf16[14,256,256]{2,1,0:T(8,128)(2,1)} %images.1, f32[2,2,32,384]{3,2,1,0:T(8,128)} %block_in.1, f32[256,512]{1,0:T(8,128)} %light.1, ...), custom_call_target="tpu_custom_call" | custom-call | tf_op jit(solution)/shard_map/exchange/pallas_call | solution.py:432
  62.9 21.9 %gradient.1 = f32[4,3,512,128]{3,2,1,0:T(8,128)} custom-call(s32[1]{0:T(128)} %get-tuple-element.15.count, s32[17]{0:T(128)} %get-tuple-element.16.slot, s32[17]{0:T(128)} %get-tuple-element.17.row, s32[17]{0:T(128)} %get-tuple-element.18.col, f32[4,3,512,128]{3,2,1,0:T(8,128)} %get-tuple-element.20.field, ...), custom_call_target="tpu_custom_call" | custom-call | tf_op jit(solution)/shard_map/gradient/pallas_call | solution.py:664
  84.8 22.5 %reduce.1 = f32[2,2,32,384]{3,2,1,0:T(8,128)} custom-call(f32[4,3,8,2,32,128]{5,4,3,2,1,0:T(8,128)} %bitcast.1, bf16[128,128]{1,0:T(8,128)(2,1)} %constant.26.unsort), custom_call_target="tpu_custom_call" | custom-call | tf_op jit(solution)/shard_map/reduce/pallas_call | solution.py:772
  107.3 1.6 %copy.17 = f32[2,2,32,384]{3,2,1,0:T(8,128)} copy(f32[2,2,32,384]{3,2,1,0:T(8,128)} %reduce.1) | data formatting | bytes 393216

commit v8 on v7

--- a/solution.py
+++ b/solution.py
@@ -222,7 +222,7 @@
 
 
 XORDER = (1, 3, 2)
-RELAY_STEPS = ((1, slice(3, 5)), (2, slice(5, 6)), (3, slice(6, 7)), (4, slice(7, 8)), (5, slice(8, 9)))
+RELAY_STEPS = ((0, slice(3, 4)), (1, slice(4, 6)), (2, slice(6, 7)), (3, slice(7, 8)), (4, slice(8, 9)))
 YORDER = (2, 1, 3)
 
 

time: 109 us -> 110 us (level)
    pallas_call x1, Pallas kernels: 21.9 us -> 24.2 us  [gradient(): pl.pallas_call(grad_kernel, out_shape=jax.ShapeDtypeStruct(field.shape, f...]
    pallas_call x1, Pallas kernels: 22.5 us -> 20.9 us  [reduce(): pl.pallas_call(functools.partial(reduce_kernel, tiles, slabs, cores), out...]
where the time goes in v8:
time: 110 us
  Pallas kernels  108 us (98%)
  local copies, waits for them, and re-layouts  1.62 us (1%)
    pallas_call x1, Pallas kernels, exchange(): pl.pallas_call(functools.partial(exchange_kernel, tiles, slabs, cores, ro...  59.9 us
    pallas_call x1, Pallas kernels, gradient(): pl.pallas_call(grad_kernel, out_shape=jax.ShapeDtypeStruct(field.shape, f...  24.2 us
    pallas_call x1, Pallas kernels, reduce(): pl.pallas_call(functools.partial(reduce_kernel, tiles, slabs, cores), out...  20.9 us
    pallas_call x1, Pallas kernels, route(): pl.pallas_call(functools.partial(route_kernel, tiles, slabs, reads), out_...  2.87 us

profile of v8, /device:TPU:1, one launch (start us, length us, event | category | flops | bytes accessed | tf_op | source)
XLA Modules:
  0.0 109.5 jit_solution(9845806468035267023)
XLA Ops:
  0.0 2.9 %route.1 = (s32[32]{0:T(128)}, s32[1]{0:T(128)}, s32[17]{0:T(128)}, s32[17]{0:T(128)}, s32[17]{0:T(128)}) custom-call(s32[1792]{0:T(1024)} %owner.1, s32[1792]{0:T(1024)} %rowoff.1, s32[1792]{0:T(1024)} %coloff.1), custom_call_target="tpu_custom_call" | custom-call | tf_op jit(solution)/shard_map/route/pallas_call | solution.py:120
  2.9 59.9 %exchange.1 = (bf16[16,2,256,256]{3,2,1,0:T(8,128)(2,1)}, f32[4,3,512,128]{3,2,1,0:T(8,128)}, f32[16,512,256]{2,1,0:T(8,128)}, f32[16,256,512]{2,1,0:T(8,128)}, f32[4,256,128]{2,1,0:T(8,128)}) custom-call(bf16[14,256,256]{2,1,0:T(8,128)(2,1)} %images.1, f32[2,2,32,384]{3,2,1,0:T(8,128)} %block_in.1, f32[256,512]{1,0:T(8,128)} %light.1, ...), custom_call_target="tpu_custom_call" | custom-call | tf_op jit(solution)/shard_map/exchange/pallas_call | solution.py:432
  62.8 24.2 %gradient.1 = f32[4,3,512,128]{3,2,1,0:T(8,128)} custom-call(s32[1]{0:T(128)} %get-tuple-element.15.count, s32[17]{0:T(128)} %get-tuple-element.16.slot, s32[17]{0:T(128)} %get-tuple-element.17.row, s32[17]{0:T(128)} %get-tuple-element.18.col, f32[4,3,512,128]{3,2,1,0:T(8,128)} %get-tuple-element.20.field, ...), custom_call_target="tpu_custom_call" | custom-call | tf_op jit(solution)/shard_map/gradient/pallas_call | solution.py:664
  87.0 20.9 %reduce.1 = f32[2,2,32,384]{3,2,1,0:T(8,128)} custom-call(f32[4,3,8,2,32,128]{5,4,3,2,1,0:T(8,128)} %bitcast.1, bf16[128,128]{1,0:T(8,128)(2,1)} %constant.26.unsort), custom_call_target="tpu_custom_call" | custom-call | tf_op jit(solution)/shard_map/reduce/pallas_call | solution.py:772
  107.9 1.6 %copy.17 = f32[2,2,32,384]{3,2,1,0:T(8,128)} copy(f32[2,2,32,384]{3,2,1,0:T(8,128)} %reduce.1) | data formatting | bytes 393216
